TPU v7x, 32 devices: a whole 2x2x4 slice. The times are simulated.
32 devices in a mesh: batch: 4 (over z), seq: 8 (over y, x, core).
Axes of the slice: x: 2, y: 2, z: 4, core: 2. Of those that a mesh axis runs over, the one named last changes fastest.
Arguments:
- tokens: bfloat16 [48, 1024, 768], P('batch', 'seq'), may hold values from -6 to 6
- attend_weight: bfloat16 [768, 2304], P('batch'), may hold values from -0.3125 to 0.3125
- query_bias: bfloat16 [768], P('batch'), may hold values from -3 to 3
- value_bias: bfloat16 [768], P('batch'), may hold values from -3 to 3
- output_weight: bfloat16 [768, 768], P('batch'), may hold values from -0.625 to 0.625
- output_bias: bfloat16 [768], P('batch'), may hold values from -3 to 3
- first_gain: bfloat16 [768], P('batch'), may hold values from 0.5 to 1.5
- first_shift: bfloat16 [768], P('batch'), may hold values from -3 to 3
- expand_weight: bfloat16 [768, 3072], P('batch'), may hold values from -0.21875 to 0.21875
- expand_bias: bfloat16 [3072], P('batch'), may hold values from -3 to 3
- reduce_weight: bfloat16 [3072, 768], P('batch'), may hold values from -0.109375 to 0.109375
- reduce_bias: bfloat16 [768], P('batch'), may hold values from -3 to 3
- second_gain: bfloat16 [768], P('batch'), may hold values from 0.5 to 1.5
- second_shift: bfloat16 [768], P('batch'), may hold values from -3 to 3
- query_rank: int32 [48, 12, 1024], P('batch', None, 'seq'), may hold values from 0 to 1023, as said below
- key_rank: int32 [48, 12, 1024], P('batch', None, 'seq'), may hold values from 0 to 1023, as said below
- cotangent: bfloat16 [48, 1024, 768], P('batch', 'seq'), may hold values from -6 to 6
Outputs:
- layer_out: bfloat16 [48, 1024, 768], P('batch', 'seq')
- token_grad: bfloat16 [48, 1024, 768], P('batch', 'seq')
- attend_weight_grad: float32 [768, 2304], P('batch')
- query_bias_grad: float32 [768], P('batch')
- value_bias_grad: float32 [768], P('batch')
- output_weight_grad: float32 [768, 768], P('batch')
- output_bias_grad: float32 [768], P('batch')
- first_gain_grad: float32 [768], P('batch')
- first_shift_grad: float32 [768], P('batch')
- expand_weight_grad: float32 [768, 3072], P('batch')
- expand_bias_grad: float32 [3072], P('batch')
- reduce_weight_grad: float32 [3072, 768], P('batch')
- reduce_bias_grad: float32 [768], P('batch')
- second_gain_grad: float32 [768], P('batch')
- second_shift_grad: float32 [768], P('batch')
Inputs may be any that keep to these rules, and one draw needn't show every extreme that they name: `query_rank`: for each sequence and head a permutation of the token places; place p lies in cluster p // 128. Of the 128 tokens of each aligned block j * 128 to (j + 1) * 128 - 1 of a sequence, exactly 16 lie in each cluster. `key_rank`: drawn independently of query_rank under the same rules.
All inputs are finite; a program needn't handle non-finite values.
Results may differ from a plain program's by a relative error of at most 0.02.
Values may be sent and summed in bfloat16 or wider, within the bound.
A program may use at most 256 MiB of HBM per device.

v0:
```python
import math

import jax
import jax.numpy as jnp
from jax import lax
from jax.sharding import PartitionSpec as P

epsilon = 1e-05


def layer_norm(resid, gain, shift):
    center = jnp.mean(resid, axis=-1, keepdims=True)
    centered = resid - center
    spread = jnp.mean(centered * centered, axis=-1, keepdims=True)
    inverse = lax.rsqrt(spread + epsilon)
    normed = centered * inverse
    return (normed * gain + shift, normed, inverse)


def norm_back(upstream, normed, inverse, gain):
    scaled = upstream * gain
    first_mean = jnp.mean(scaled, axis=-1, keepdims=True)
    second_mean = jnp.mean(scaled * normed, axis=-1, keepdims=True)
    return inverse * (scaled - first_mean - normed * second_mean)


def gelu_slope(value):
    cumulative = 0.5 * (1.0 + lax.erf(value * 0.5**0.5))
    density = jnp.exp(-0.5 * value * value) * (2.0 * math.pi) ** (-0.5)
    return cumulative + value * density


def transpose_left(first, second):
    return lax.dot_general(
        first, second, (((0,), (0,)), ((), ())), preferred_element_type=jnp.float32
    )


def transpose_right(first, second):
    return lax.dot_general(
        first, second, (((1,), (1,)), ((), ())), preferred_element_type=jnp.float32
    )


def group_table(rank, cluster, owners):
    share = cluster // owners
    target = rank // cluster
    length = rank.shape[-1]
    places = lax.broadcasted_iota(jnp.int32, (length, length), 0)
    later = lax.broadcasted_iota(jnp.int32, (length, length), 1)
    before = (places < later)[None, None]
    same = target[..., :, None] == target[..., None, :]
    earlier = jnp.sum((same & before).astype(jnp.int32), axis=-2)
    position = target * share + earlier
    slots = lax.broadcasted_iota(jnp.int32, position.shape + (length,), 3)
    return (position[..., None] == slots).astype(jnp.bfloat16)


def sort_heads(rows, table, heads):
    seqs, length, width = rows.shape
    split = rows.reshape(seqs, length, heads, width // heads)
    moved = jnp.einsum("shtp,sthd->sphd", table, split, preferred_element_type=jnp.float32)
    return moved.astype(rows.dtype).reshape(seqs, length, width)


def unsort_heads(rows, table, heads):
    seqs, length, width = rows.shape
    split = rows.reshape(seqs, length, heads, width // heads)
    moved = jnp.einsum("shtp,sphd->sthd", table, split, preferred_element_type=jnp.float32)
    return moved.astype(rows.dtype).reshape(seqs, length, width)


def cluster_scores(queries, keys_rows, heads):
    items, length, width = queries.shape
    size = width // heads
    query_split = queries.reshape(items, length, heads, size)
    key_split = keys_rows.reshape(items, length, heads, size)
    scores = jnp.einsum(
        "sqhd,skhd->shqk", query_split, key_split, preferred_element_type=jnp.float32
    )
    return scores * size ** (-0.5)


def cluster_forward(queries, keys_rows, values_rows, heads):
    items, length, width = queries.shape
    scores = cluster_scores(queries, keys_rows, heads)
    top = jnp.max(scores, axis=-1, keepdims=True)
    weights = jnp.exp(scores - top)
    total = jnp.sum(weights, axis=-1, keepdims=True)
    probs = (weights / total).astype(jnp.bfloat16)
    value_split = values_rows.reshape(items, length, heads, width // heads)
    context = jnp.einsum("shqk,skhd->sqhd", probs, value_split, preferred_element_type=jnp.float32)
    return (
        context.reshape(items, length, width).astype(jnp.bfloat16),
        (top + jnp.log(total))[..., 0],
    )


def cluster_backward(scores, log_total, queries, keys_rows, values_rows, grad_context, heads):
    items, length, width = queries.shape
    size = width // heads
    query_split = queries.reshape(items, length, heads, size)
    key_split = keys_rows.reshape(items, length, heads, size)
    value_split = values_rows.reshape(items, length, heads, size)
    grad_split = grad_context.reshape(items, length, heads, size)
    probs = jnp.exp(scores - log_total[..., None])
    grad_probs = jnp.einsum(
        "sqhd,skhd->shqk", grad_split, value_split, preferred_element_type=jnp.float32
    )
    inner = jnp.sum(probs * grad_probs, axis=-1, keepdims=True)
    grad_scores = (probs * (grad_probs - inner)).astype(jnp.bfloat16)
    scale = size ** (-0.5)
    grad_query = (
        jnp.einsum("shqk,skhd->sqhd", grad_scores, key_split, preferred_element_type=jnp.float32)
        * scale
    )
    grad_key = (
        jnp.einsum("shqk,sqhd->skhd", grad_scores, query_split, preferred_element_type=jnp.float32)
        * scale
    )
    grad_value = jnp.einsum(
        "shqk,sqhd->skhd",
        probs.astype(jnp.bfloat16),
        grad_split,
        preferred_element_type=jnp.float32,
    )
    shape = (items, length, width)
    return (
        grad_query.reshape(shape).astype(jnp.bfloat16),
        grad_key.reshape(shape).astype(jnp.bfloat16),
        grad_value.reshape(shape).astype(jnp.bfloat16),
    )


def send_context(context):
    return lax.all_to_all(context, "seq", split_axis=1, concat_axis=1, tiled=True)


def send_grads(grads):
    return (
        lax.all_to_all(grads[0], "seq", split_axis=1, concat_axis=1, tiled=True),
        lax.all_to_all(grads[1], "seq", split_axis=1, concat_axis=1, tiled=True),
        lax.all_to_all(grads[2], "seq", split_axis=1, concat_axis=1, tiled=True),
    )


def make_step(left, pieces):
    total = jnp.dot(left, pieces[0], preferred_element_type=jnp.float32)
    stored = tuple(pieces[1:]) + ()
    placed = tuple((piece for piece in stored))
    return (total,) + placed


def make_hidden_step(before, pieces):
    section = before + pieces[1].astype(jnp.float32)
    activated = jax.nn.gelu(section, approximate=False).astype(jnp.bfloat16)
    total = jnp.dot(activated, pieces[0], preferred_element_type=jnp.float32)
    stored = ()
    return (total, section, activated) + stored


def per_device(
    tokens,
    attend_weight,
    query_bias,
    value_bias,
    output_weight,
    output_bias,
    first_gain,
    first_shift,
    expand_weight,
    expand_bias,
    reduce_weight,
    reduce_bias,
    second_gain,
    second_shift,
    query_rank,
    key_rank,
    cotangent,
):
    seqs, cluster, width = tokens.shape
    heads = query_rank.shape[1]
    rows = seqs * cluster
    owners = lax.axis_size("seq")
    flat = tokens.reshape(rows, width)
    attend_out = make_step(
        flat,
        (
            lax.all_gather(attend_weight, "batch", axis=0, tiled=True),
            lax.all_gather(query_bias, "batch", axis=0, tiled=True),
            lax.all_gather(value_bias, "batch", axis=0, tiled=True),
        ),
    )
    summed = attend_out[0]
    queries = (summed[:, :width] + attend_out[1].astype(jnp.float32)).astype(jnp.bfloat16)
    keys_rows = summed[:, width : 2 * width].astype(jnp.bfloat16)
    values_rows = (summed[:, 2 * width :] + attend_out[2].astype(jnp.float32)).astype(jnp.bfloat16)
    query_table = group_table(query_rank, cluster, owners)
    key_table = group_table(key_rank, cluster, owners)
    query_sorted = sort_heads(queries.reshape(seqs, cluster, width), query_table, heads)
    key_sorted = sort_heads(keys_rows.reshape(seqs, cluster, width), key_table, heads)
    value_sorted = sort_heads(values_rows.reshape(seqs, cluster, width), key_table, heads)
    received = (
        lax.all_to_all(query_sorted, "seq", split_axis=1, concat_axis=1, tiled=True),
        lax.all_to_all(key_sorted, "seq", split_axis=1, concat_axis=1, tiled=True),
        lax.all_to_all(value_sorted, "seq", split_axis=1, concat_axis=1, tiled=True),
    )
    context, log_total = cluster_forward(received[0], received[1], received[2], heads)
    forward_out = (send_context(context), log_total, received[0], received[1], received[2])
    context_rows = unsort_heads(forward_out[0], query_table, heads).reshape(rows, width)
    output_out = make_step(
        context_rows,
        (
            lax.all_gather(output_weight, "batch", axis=0, tiled=True),
            lax.all_gather(output_bias, "batch", axis=0, tiled=True),
            lax.all_gather(first_gain, "batch", axis=0, tiled=True),
            lax.all_gather(first_shift, "batch", axis=0, tiled=True),
        ),
    )
    resid_one = flat.astype(jnp.float32) + output_out[0] + output_out[1].astype(jnp.float32)
    gain_one = output_out[2].astype(jnp.float32)
    middle, normed_one, inverse_one = layer_norm(
        resid_one, gain_one, output_out[3].astype(jnp.float32)
    )
    middle_low = middle.astype(jnp.bfloat16)
    expand_out = make_step(
        middle_low,
        (
            lax.all_gather(expand_weight, "batch", axis=0, tiled=True),
            lax.all_gather(reduce_bias, "batch", axis=0, tiled=True),
            lax.all_gather(second_gain, "batch", axis=0, tiled=True),
            lax.all_gather(second_shift, "batch", axis=0, tiled=True),
        ),
    )
    hidden_out = make_hidden_step(
        expand_out[0],
        (
            lax.all_gather(reduce_weight, "batch", axis=0, tiled=True),
            lax.all_gather(expand_bias, "batch", axis=0, tiled=True),
        ),
    )
    pre_full, hidden_full = (hidden_out[1], hidden_out[2])
    resid_two = middle + hidden_out[0] + expand_out[1].astype(jnp.float32)
    gain_two = expand_out[2].astype(jnp.float32)
    final, normed_two, inverse_two = layer_norm(
        resid_two, gain_two, expand_out[3].astype(jnp.float32)
    )
    layer_out = final.astype(jnp.bfloat16).reshape(seqs, cluster, width)
    attend_full, output_full, expand_full, reduce_full = (
        lax.all_gather(attend_weight, "batch", axis=0, tiled=True),
        lax.all_gather(output_weight, "batch", axis=0, tiled=True),
        lax.all_gather(expand_weight, "batch", axis=0, tiled=True),
        lax.all_gather(reduce_weight, "batch", axis=0, tiled=True),
    )
    upstream = cotangent.reshape(rows, width).astype(jnp.float32)
    grad_second_gain = jnp.sum(upstream * normed_two, axis=0)
    grad_second_shift = jnp.sum(upstream, axis=0)
    grad_resid_two = norm_back(upstream, normed_two, inverse_two, gain_two)
    grad_branch_two = grad_resid_two.astype(jnp.bfloat16)
    grad_reduce_bias = jnp.sum(grad_branch_two, axis=0, dtype=jnp.float32)
    grad_reduce = transpose_left(hidden_full, grad_branch_two)
    grad_hidden = transpose_right(grad_branch_two, reduce_full)
    grad_pre = (grad_hidden * gelu_slope(pre_full)).astype(jnp.bfloat16)
    grad_expand_bias = jnp.sum(grad_pre, axis=0, dtype=jnp.float32)
    grad_expand = transpose_left(middle_low, grad_pre)
    grad_middle = grad_resid_two + transpose_right(grad_pre, expand_full)
    grad_first_gain = jnp.sum(grad_middle * normed_one, axis=0)
    grad_first_shift = jnp.sum(grad_middle, axis=0)
    grad_resid_one = norm_back(grad_middle, normed_one, inverse_one, gain_one)
    grad_branch_one = grad_resid_one.astype(jnp.bfloat16)
    grad_output_bias = jnp.sum(grad_branch_one, axis=0, dtype=jnp.float32)
    grad_output = transpose_left(context_rows, grad_branch_one)
    grad_context = transpose_right(grad_branch_one, output_full).astype(jnp.bfloat16)
    grad_sorted = sort_heads(grad_context.reshape(seqs, cluster, width), query_table, heads)
    grad_received = lax.all_to_all(grad_sorted, "seq", split_axis=1, concat_axis=1, tiled=True)
    kept_scores = cluster_scores(forward_out[2], forward_out[3], heads)
    home = send_grads(
        cluster_backward(
            kept_scores,
            forward_out[1],
            forward_out[2],
            forward_out[3],
            forward_out[4],
            grad_received,
            heads,
        )
    )
    grad_queries = unsort_heads(home[0], query_table, heads).reshape(rows, width)
    grad_keys = unsort_heads(home[1], key_table, heads).reshape(rows, width)
    grad_values = unsort_heads(home[2], key_table, heads).reshape(rows, width)
    grad_mixed = jnp.concatenate([grad_queries, grad_keys, grad_values], axis=1)
    grad_query_bias = jnp.sum(grad_queries, axis=0, dtype=jnp.float32)
    grad_value_bias = jnp.sum(grad_values, axis=0, dtype=jnp.float32)
    grad_attend = transpose_left(flat, grad_mixed)
    token_grad = (
        (grad_resid_one + transpose_right(grad_mixed, attend_full))
        .astype(jnp.bfloat16)
        .reshape(seqs, cluster, width)
    )
    owned = (
        lax.psum_scatter(
            grad_attend.astype(jnp.bfloat16), "batch", scatter_dimension=0, tiled=True
        ).astype(jnp.float32),
        lax.psum_scatter(
            grad_query_bias.astype(jnp.bfloat16), "batch", scatter_dimension=0, tiled=True
        ).astype(jnp.float32),
        lax.psum_scatter(
            grad_value_bias.astype(jnp.bfloat16), "batch", scatter_dimension=0, tiled=True
        ).astype(jnp.float32),
        lax.psum_scatter(
            grad_output.astype(jnp.bfloat16), "batch", scatter_dimension=0, tiled=True
        ).astype(jnp.float32),
        lax.psum_scatter(
            grad_output_bias.astype(jnp.bfloat16), "batch", scatter_dimension=0, tiled=True
        ).astype(jnp.float32),
        lax.psum_scatter(
            grad_first_gain.astype(jnp.bfloat16), "batch", scatter_dimension=0, tiled=True
        ).astype(jnp.float32),
        lax.psum_scatter(
            grad_first_shift.astype(jnp.bfloat16), "batch", scatter_dimension=0, tiled=True
        ).astype(jnp.float32),
        lax.psum_scatter(
            grad_expand.astype(jnp.bfloat16), "batch", scatter_dimension=0, tiled=True
        ).astype(jnp.float32),
        lax.psum_scatter(
            grad_expand_bias.astype(jnp.bfloat16), "batch", scatter_dimension=0, tiled=True
        ).astype(jnp.float32),
        lax.psum_scatter(
            grad_reduce.astype(jnp.bfloat16), "batch", scatter_dimension=0, tiled=True
        ).astype(jnp.float32),
        lax.psum_scatter(
            grad_reduce_bias.astype(jnp.bfloat16), "batch", scatter_dimension=0, tiled=True
        ).astype(jnp.float32),
        lax.psum_scatter(
            grad_second_gain.astype(jnp.bfloat16), "batch", scatter_dimension=0, tiled=True
        ).astype(jnp.float32),
        lax.psum_scatter(
            grad_second_shift.astype(jnp.bfloat16), "batch", scatter_dimension=0, tiled=True
        ).astype(jnp.float32),
    )
    shared = (
        lax.psum(owned[0].astype(jnp.bfloat16), "seq").astype(jnp.float32),
        lax.psum(owned[1].astype(jnp.bfloat16), "seq").astype(jnp.float32),
        lax.psum(owned[2].astype(jnp.bfloat16), "seq").astype(jnp.float32),
        lax.psum(owned[3].astype(jnp.bfloat16), "seq").astype(jnp.float32),
        lax.psum(owned[4].astype(jnp.bfloat16), "seq").astype(jnp.float32),
        lax.psum(owned[5].astype(jnp.bfloat16), "seq").astype(jnp.float32),
        lax.psum(owned[6].astype(jnp.bfloat16), "seq").astype(jnp.float32),
        lax.psum(owned[7].astype(jnp.bfloat16), "seq").astype(jnp.float32),
        lax.psum(owned[8].astype(jnp.bfloat16), "seq").astype(jnp.float32),
        lax.psum(owned[9].astype(jnp.bfloat16), "seq").astype(jnp.float32),
        lax.psum(owned[10].astype(jnp.bfloat16), "seq").astype(jnp.float32),
        lax.psum(owned[11].astype(jnp.bfloat16), "seq").astype(jnp.float32),
        lax.psum(owned[12].astype(jnp.bfloat16), "seq").astype(jnp.float32),
    )
    return (
        layer_out,
        token_grad,
        shared[0],
        shared[1],
        shared[2],
        shared[3],
        shared[4],
        shared[5],
        shared[6],
        shared[7],
        shared[8],
        shared[9],
        shared[10],
        shared[11],
        shared[12],
    )


def solution(mesh):
    in_specs = (
        P("batch", "seq", None),
        P("batch", None),
        P("batch"),
        P("batch"),
        P("batch", None),
        P("batch"),
        P("batch"),
        P("batch"),
        P("batch", None),
        P("batch"),
        P("batch", None),
        P("batch"),
        P("batch"),
        P("batch"),
        P("batch", None, "seq"),
        P("batch", None, "seq"),
        P("batch", "seq", None),
    )
    out_specs = (
        P("batch", "seq", None),
        P("batch", "seq", None),
        P("batch", None),
        P("batch"),
        P("batch"),
        P("batch", None),
        P("batch"),
        P("batch"),
        P("batch"),
        P("batch", None),
        P("batch"),
        P("batch", None),
        P("batch"),
        P("batch"),
        P("batch"),
    )
    return jax.shard_map(
        per_device, mesh=mesh, in_specs=in_specs, out_specs=out_specs, check_vma=False
    )
```

profile of v0, /device:TPU:0, one launch (start us, length us, event | category | flops | bytes accessed | tf_op | source)
XLA Modules:
  0.0 1056.4 jit_solution(10841457245450229804)
XLA Ops:
  15.8 21.7 %all-reduce.20 = (bf16[768]{0:T(1024)(128)(2,1)S(1)}, bf16[768]{0:T(1024)(128)(2,1)S(1)}, bf16[768]{0:T(1024)(128)(2,1)S(1)}, bf16[768]{0:T(1024)(128)(2,1)S(1)}...) all-reduce(bf16[768]{0:T(1024)(128)(2,1)S(1)} %dynamic-update-slice, ...), channel_id=1, replica_groups=mesh['batch'=4,'seq'=8] {'batch'}, use_global_device_ids=true, to_apply=%add.2 | all-reduce | flops 5376 | bytes 21504
  45.8 36.7 %all-gather.6.cloned.1.call-done = bf16[768,2304]{1,0:T(8,128)(2,1)} async-done(((bf16[192,2304]{1,0:T(8,128)(2,1)}), bf16[768,2304]{1,0:T(8,128)(2,1)}) %all-gather.6.cloned.1.call-update) | async-done | bytes 3538960 | tf_op jit(solution)/shard_map/all_gather | solution.py:189
  82.5 8.5 fusion.98
  118.1 8.2 reshape.236
  126.3 8.3 fusion.67
  139.4 15.6 %all-to-all-done = bf16[12,128,768]{2,0,1:T(8,128)(2,1)S(1)} async-done(((bf16[12,128,768]{2,0,1:T(8,128)(2,1)}), bf16[12,128,768]{2,0,1:T(8,128)(2,1)S(1)}, u32[]{:S(2)}, u32[]{:S(2)}) %all-to-all-start) | async-done | bytes 2359328 | tf_op jit(solution)/shard_map/all_to_all | solution.py:206
  164.3 8.2 reshape.237
  172.5 8.2 fusion.64
  185.6 11.9 %all-to-all-done.1 = bf16[12,128,768]{2,0,1:T(8,128)(2,1)} async-done(((bf16[12,128,768]{2,0,1:T(8,128)(2,1)}), bf16[12,128,768]{2,0,1:T(8,128)(2,1)}, u32[]{:S(2)}, u32[]{:S(2)}) %all-to-all-start.1) | async-done | bytes 2359328 | tf_op jit(solution)/shard_map/all_to_all | solution.py:204
  209.1 30.8 %all-to-all-done.2 = bf16[12,128,768]{2,0,1:T(8,128)(2,1)} async-done(((bf16[12,128,768]{2,0,1:T(8,128)(2,1)}), bf16[12,128,768]{2,0,1:T(8,128)(2,1)}, u32[]{:S(2)}, u32[]{:S(2)}) %all-to-all-start.2) | async-done | bytes 2359328 | tf_op jit(solution)/shard_map/all_to_all | solution.py:205
  263.7 26.5 %all-gather = bf16[4,1,768]{2,1,0:T(2,128)(2,1)S(1)} all-gather(bf16[1,1,768]{2,1,0:T(2,128)(2,1)S(1)} %reshape.216), channel_id=1, replica_groups=mesh['batch'=4,'seq'=8] {'batch'}, dimensions={0}, use_global_device_ids=true | all-gather | bytes 7680 | tf_op jit(solution)/shard_map/all_gather | solution.py:239
  291.4 9.5 all-to-all-done.3
  321.0 52.9 %fusion.2 = (bf16[1536,3072]{1,0:T(8,128)(2,1)}, f32[1536,3072]{1,0:T(8,128)}) fusion(f32[3072]{0:T(1024)S(1)} %bitcast.159, bf16[768,3072]{1,0:T(8,128)(2,1)} %all-gather.10.cloned.1.call-done, f32[1536,768]{1,0:T(8,128)} %copy-done.7, f32[768]{0:T(1024)S(1)} %convert_element_type.292, f32[768]{0:T(1024)S(1)} %convert_element_type.291, ...), kind=kOutput, calls=%fused_computation.4 | convolution fusion | flops 7565082624 | bytes 37779456 | tf_op jit(solution)/shard_map/dot_general | solution.py:148
  373.9 13.2 %fusion.94 = (f32[1536]{0:T(1024)S(1)}, f32[1536,768]{1,0:T(8,128)S(1)}) fusion(f32[768]{0:T(1024)S(1)} %convert_element_type.296, bf16[1536,3072]{1,0:T(8,128)(2,1)} %get-tuple-element.125, bf16[3072,768]{1,0:T(8,128)(2,1)} %all-gather.12.cloned.1.call-done, f32[768]{0:T(1024)S(1)} %convert_element_type.292, f32[768]{0:T(1024)S(1)} %convert_element_type.291, ...), kind=kOutput, calls=%fused_computation.155 | convolution fusion | flops 7256013312 | bytes 23620608 | tf_op jit(solution)/shard_map/dot_general | solution.py:157
  395.7 20.8 %fusion.97 = (bf16[3072]{0:T(1024)(128)(2,1)}, bf16[1536,3072]{1,0:T(8,128)(2,1)}) fusion(f32[1536,3072]{1,0:T(8,128)} %get-tuple-element.126, f32[3072]{0:T(1024)S(1)} %bitcast.160, bf16[3072,768]{1,0:T(8,128)(2,1)S(1)} %bitcast.162, f32[1536,768]{1,0:T(8,128)S(1)} %get-tuple-element.114), kind=kOutput, calls=%fused_computation.158 | convolution fusion | flops 7305556992 | bytes 37767168 | tf_op jit(solution)/shard_map/dot_general | solution.py:40
  416.5 13.6 %multiply_reduce_fusion.2 = (bf16[768]{0:T(1024)(128)(2,1)}, f32[1536]{0:T(1024)S(1)}, f32[1536]{0:T(1024)S(1)}, bf16[768]{0:T(1024)(128)(2,1)}, f32[1536,768]{1,0:T(8,128)S(1)}) fusion(f32[1536,768]{1,0:T(8,128)S(1)} %bitcast.136, f32[1536]{0:T(1024)S(1)} %add_rsqrt_fusion.1, f32[1536]{0:T(1024)S(1)} %broadcast_multiply_fusion.4, ...), kind=kOutput, calls=%fused_computation.69 | convolution fusion | flops 7259548672 | bytes 28342272 | tf_op jit(solution)/shard_map/dot_general | solution.py:40
  458.3 37.8 %all-to-all-done.4 = bf16[12,128,768]{2,0,1:T(8,128)(2,1)} async-done(((bf16[12,128,768]{2,0,1:T(8,128)(2,1)}), bf16[12,128,768]{2,0,1:T(8,128)(2,1)}, u32[]{:S(2)}, u32[]{:S(2)}) %all-to-all-start.4) | async-done | bytes 2359328 | tf_op jit(solution)/shard_map/all_to_all | solution.py:275
  500.1 10.6 %multiply_reduce_fusion = (f32[12,12,128]{2,1,0:T(8,128)S(1)}, f32[12,12,128,128]{2,3,1,0:T(8,128)}) fusion(f32[12,12,128,128]{2,3,1,0:T(8,128)} %copy-done, f32[12,12,128]{2,1,0:T(8,128)S(1)} %log_add_fusion, bf16[12,128,12,64]{1,3,2,0:T(8,128)(2,1)S(1)} %bitcast.129, bf16[12,128,12,64]{1,3,2,0:T(8,128)(2,1)} %bitcast.140), kind=kOutput, calls=%fused_computation.27 | convolution fusion | flops 311408640 | bytes 23740416 | tf_op jit(solution)/shard_map/sqhd,skhd->shqk/dot_general | solution.py:107
  510.6 11.4 %multiply_convert_fusion = bf16[12,12,128,128]{2,3,1,0:T(8,128)(2,1)} fusion(f32[12,12,128,128]{2,3,1,0:T(8,128)} %get-tuple-element.131, f32[12,12,128,128]{2,3,1,0:T(8,128)} %copy-done, f32[12,12,128]{2,1,0:T(8,128)S(1)} %get-tuple-element.130, f32[12,12,128]{2,1,0:T(8,128)S(1)} %log_add_fusion), kind=kLoop, calls=%fused_computation.26 | loop fusion | flops 11796480 | bytes 23740416 | tf_op jit(solution)/shard_map/convert_element_type | solution.py:111
  537.6 8.4 fusion.58
  551.1 24.4 %all-to-all-done.5 = bf16[12,128,768]{2,0,1:T(8,128)(2,1)} async-done(((bf16[12,128,768]{2,0,1:T(8,128)(2,1)}), bf16[12,128,768]{2,0,1:T(8,128)(2,1)}, u32[]{:S(2)}, u32[]{:S(2)}) %all-to-all-start.5) | async-done | bytes 2359328 | tf_op jit(solution)/shard_map/all_to_all | solution.py:141
  592.0 25.9 %all-to-all-done.7 = bf16[12,128,768]{2,0,1:T(8,128)(2,1)} async-done(((bf16[12,128,768]{2,0,1:T(8,128)(2,1)}), bf16[12,128,768]{2,0,1:T(8,128)(2,1)}, u32[]{:S(2)}, u32[]{:S(2)}) %all-to-all-start.7) | async-done | bytes 2359328 | tf_op jit(solution)/shard_map/all_to_all | solution.py:143
  641.6 8.1 fusion.96
  693.5 14.1 %convolution_convert_fusion.2 = bf16[768,3072]{1,0:T(8,128)(2,1)} fusion(bf16[1536,3072]{1,0:T(8,128)(2,1)} %get-tuple-element.137, f32[1536,768]{1,0:T(8,128)} %copy-done.7, f32[768]{0:T(1024)S(1)} %copy-done.41, f32[768]{0:T(1024)S(1)} %copy-done.35, f32[1536]{0:T(1024)S(1)} %add_rsqrt_fusion.1, f32[1536]{0:T(1024)S(1)} %broadcast_multiply_fusion.4), kind=kOutput, calls=%fused_computation.48 | convolution fusion | flops 7256014848 | bytes 18892800 | tf_op jit(solution)/shard_map/dot_general | solution.py:34
  707.7 13.2 %convolution_convert_fusion = bf16[3072,768]{1,0:T(8,128)(2,1)} fusion(bf16[1536,3072]{1,0:T(8,128)(2,1)} %get-tuple-element.125, f32[1536,768]{1,0:T(8,128)} %copy-done.11), kind=kOutput, calls=%fused_computation.46 | convolution fusion | flops 7251296256 | bytes 18874368 | tf_op jit(solution)/shard_map/dot_general | solution.py:34
  724.7 20.2 %all-reduce.19 = (bf16[768]{0:T(1024)(128)(2,1)S(1)}, bf16[768]{0:T(1024)(128)(2,1)S(1)}, bf16[768]{0:T(1024)(128)(2,1)S(1)}, bf16[768]{0:T(1024)(128)(2,1)S(1)}...) all-reduce(bf16[768]{0:T(1024)(128)(2,1)S(1)} %dynamic-update-slice, ...), channel_id=1, replica_groups=mesh['batch'=4,'seq'=8] {'batch'}, use_global_device_ids=true, to_apply=%add.7 | all-reduce | flops 9984 | bytes 39936
  745.6 12.4 %all-reduce.17 = (bf16[192]{0:T(256)(128)(2,1)S(1)}, bf16[192]{0:T(256)(128)(2,1)S(1)}, bf16[192]{0:T(256)(128)(2,1)S(1)}, bf16[192]{0:T(256)(128)(2,1)S(1)}, bf...) all-reduce(bf16[192]{0:T(256)(128)(2,1)S(1)} %dynamic-slice.9, ...), channel_id=1, replica_groups=mesh['batch'=4,'seq'=8] {'seq'}, use_global_device_ids=true, to_apply=%region_17.18 | all-reduce | flops 2304 | bytes 9216 | tf_op jit(solution)/shard_map/psum | solution.py:343
  769.5 13.9 %reduce-scatter.7.cloned.1.call-done = bf16[192,768]{1,0:T(8,128)(2,1)} async-done(((bf16[768,768]{1,0:T(8,128)(2,1)}), bf16[192,768]{1,0:T(8,128)(2,1)}) %reduce-scatter.7.cloned.1.call-update) | async-done | bytes 294928 | tf_op jit(solution)/shard_map/reduce_scatter | solution.py:310
  783.4 86.3 %reduce-scatter.9.cloned.1.call-done = bf16[192,3072]{1,0:T(8,128)(2,1)} async-done(((bf16[768,3072]{1,0:T(8,128)(2,1)}), bf16[192,3072]{1,0:T(8,128)(2,1)}) %reduce-scatter.9.cloned.1.call-update) | async-done | bytes 1179664 | tf_op jit(solution)/shard_map/reduce_scatter | solution.py:322
  869.7 88.1 %reduce-scatter.11.cloned.1.call-done = bf16[768,768]{1,0:T(8,128)(2,1)} async-done(((bf16[3072,768]{1,0:T(8,128)(2,1)}), bf16[768,768]{1,0:T(8,128)(2,1)}) %reduce-scatter.11.cloned.1.call-update) | async-done | bytes 1179664 | tf_op jit(solution)/shard_map/reduce_scatter | solution.py:328
  957.8 10.6 %add_convert_fusion = bf16[1536,768]{1,0:T(8,128)(2,1)} fusion(f32[1536,768]{1,0:T(8,128)} %copy-done.12, bf16[1536,2304]{0,1:T(8,128)(2,1)} %copy-done.18, bf16[768,2304]{1,0:T(8,128)(2,1)S(1)} %copy-done.48), kind=kOutput, calls=%fused_computation.70 | convolution fusion | flops 5438177280 | bytes 17694720 | tf_op jit(solution)/shard_map/dot_general | solution.py:40
  968.4 72.3 %all-reduce.23.cloned.1.call-done = (bf16[192,2304]{0,1:T(8,128)(2,1)}, bf16[192,768]{1,0:T(8,128)(2,1)}, bf16[192,3072]{1,0:T(8,128)(2,1)}, bf16[768,768]{1,0:T(8,128)(2,1)}) async-done(((bf16[192,2304]{0,1:T(8,128)(2,1)}, bf16[192,768]{1,0:T(8,128)(2,1)}, bf16[192,3072]{1,0:T(8,128)(2,1)}, bf16[768,768]{1,0:T(8,128)(2,1)}), (bf16[192,2304]{0,1:T(8,128)(2,1)}, bf16[192,768]{1,0:T(8,128)(2,1)}, ...) | async-done | bytes 3538960 | tf_op jit(solution)/shard_map/psum | solution.py:342
  (266 shorter events, 287.1 us)
Async XLA Ops:
  7.2 75.3 %all-gather.6.cloned.1.call-start = ((), (), s32[]{:S(2)}) async-start(), calls=%async_computation.12 | async-start | bytes 4423680 | tf_op jit(solution)/shard_map/all_gather | solution.py:189
  45.8 126.7 %copy-start.29 = (s32[12,12,128]{2,1,0:T(8,128)}, s32[12,12,128]{2,1,0:T(8,128)S(1)}, u32[]{:S(2)}) copy-start(s32[12,12,128]{2,1,0:T(8,128)S(1)} %multiply_add_fusion.2) | copy-start | bytes 221188
  113.6 41.5 %all-to-all-start = ((bf16[12,128,768]{2,0,1:T(8,128)(2,1)}), bf16[12,128,768]{2,0,1:T(8,128)(2,1)S(1)}, u32[]{:S(2)}, u32[]{:S(2)}) async-start(bf16[12,128,768]{2,0,1:T(8,128)(2,1)} %copy.93), calls=%async_computation | async-start | bytes 6291456 | tf_op jit(solution)/shard_map/all_to_all | solution.py:206
  117.2 195.1 %all-gather.8.cloned.1.call-start = ((), (), s32[]{:S(2)}) async-start(), calls=%async_computation.13 | async-start | bytes 1474560 | tf_op jit(solution)/shard_map/all_gather | solution.py:214
  118.0 186.9 %copy-start.31 = (s32[12,12,128]{2,1,0:T(8,128)}, s32[12,12,128]{2,1,0:T(8,128)S(1)}, u32[]{:S(2)}) copy-start(s32[12,12,128]{2,1,0:T(8,128)S(1)} %multiply_add_fusion.1) | copy-start | bytes 221188
  155.1 42.4 %all-to-all-start.1 = ((bf16[12,128,768]{2,0,1:T(8,128)(2,1)}), bf16[12,128,768]{2,0,1:T(8,128)(2,1)}, u32[]{:S(2)}, u32[]{:S(2)}) async-start(bf16[12,128,768]{2,0,1:T(8,128)(2,1)} %copy.97), calls=%async_computation.1 | async-start | bytes 6291456 | tf_op jit(solution)/shard_map/all_to_all | solution.py:204
  159.6 161.4 %all-gather.10.cloned.1.call-start = ((), (), s32[]{:S(2)}) async-start(), calls=%async_computation.14 | async-start | bytes 5898240 | tf_op jit(solution)/shard_map/all_gather | solution.py:229
  197.5 42.4 %all-to-all-start.2 = ((bf16[12,128,768]{2,0,1:T(8,128)(2,1)}), bf16[12,128,768]{2,0,1:T(8,128)(2,1)}, u32[]{:S(2)}, u32[]{:S(2)}) async-start(bf16[12,128,768]{2,0,1:T(8,128)(2,1)} %copy.101), calls=%async_computation.2 | async-start | bytes 6291456 | tf_op jit(solution)/shard_map/all_to_all | solution.py:205
  209.0 39.0 %copy-start.5 = (bf16[12,128,768]{1,2,0:T(8,128)(2,1)}, bf16[12,128,768]{1,2,0:T(8,128)(2,1)S(1)}, u32[]{:S(2)}) copy-start(bf16[12,128,768]{1,2,0:T(8,128)(2,1)S(1)} %copy.98) | copy-start | bytes 7077892
  258.5 31.8 %copy-start.2 = (bf16[12,128,768]{2,1,0:T(8,128)(2,1)S(1)}, bf16[12,128,768]{2,1,0:T(8,128)(2,1)}, u32[]{:S(2)}) copy-start(bf16[12,128,768]{2,1,0:T(8,128)(2,1)} %param.33) | copy-start | bytes 7077892
  258.5 42.5 %all-to-all-start.3 = ((bf16[12,128,768]{2,0,1:T(8,128)(2,1)}), bf16[12,128,768]{2,0,1:T(8,128)(2,1)}, u32[]{:S(2)}, u32[]{:S(2)}) async-start(bf16[12,128,768]{2,0,1:T(8,128)(2,1)} %copy.104), calls=%async_computation.3 | async-start | bytes 6291456 | tf_op jit(solution)/shard_map/all_to_all | solution.py:136
  263.1 110.9 %all-gather.12.cloned.1.call-start = ((), (), s32[]{:S(2)}) async-start(), calls=%async_computation.15 | async-start | bytes 5898240 | tf_op jit(solution)/shard_map/all_gather | solution.py:238
  290.2 83.7 %copy-start.40 = (f32[768]{0:T(1024)}, f32[768]{0:T(1024)S(1)}, u32[]{:S(2)}) copy-start(f32[768]{0:T(1024)S(1)} %convert_element_type.292) | copy-start | bytes 9220
  290.2 139.9 %copy-start.34 = (f32[768]{0:T(1024)}, f32[768]{0:T(1024)S(1)}, u32[]{:S(2)}) copy-start(f32[768]{0:T(1024)S(1)} %convert_element_type.291) | copy-start | bytes 9220
  393.3 23.2 %slice-start = ((s8[4718592]{0:T(1024)(128)(4,1)}), s8[4194304]{0:T(1024)(128)(4,1)S(1)}, s32[]{:S(2)}) async-start(s8[4718592]{0:T(1024)(128)(4,1)} %bitcast.135), calls=%async_computation.21 | async-start | bytes 8388608
  395.7 20.8 %copy-start.11 = (f32[1536,768]{1,0:T(8,128)}, f32[1536,768]{1,0:T(8,128)S(1)}, u32[]{:S(2)}) copy-start(f32[1536,768]{1,0:T(8,128)S(1)} %get-tuple-element.114) | copy-start | bytes 14155780
  395.7 20.8 %slice-start.1 = ((s8[4718592]{0:T(1024)(128)(4,1)}), s8[524288]{0:T(1024)(128)(4,1)S(1)}, s32[]{:S(2)}) async-start(s8[4718592]{0:T(1024)(128)(4,1)} %bitcast.135), calls=%async_computation.22 | async-start | bytes 1048576
  453.7 42.4 %all-to-all-start.4 = ((bf16[12,128,768]{2,0,1:T(8,128)(2,1)}), bf16[12,128,768]{2,0,1:T(8,128)(2,1)}, u32[]{:S(2)}, u32[]{:S(2)}) async-start(bf16[12,128,768]{2,0,1:T(8,128)(2,1)} %copy.109), calls=%async_computation.4 | async-start | bytes 6291456 | tf_op jit(solution)/shard_map/all_to_all | solution.py:275
  532.8 42.8 %all-to-all-start.5 = ((bf16[12,128,768]{2,0,1:T(8,128)(2,1)}), bf16[12,128,768]{2,0,1:T(8,128)(2,1)}, u32[]{:S(2)}, u32[]{:S(2)}) async-start(bf16[12,128,768]{2,0,1:T(8,128)(2,1)} %copy.112), calls=%async_computation.5 | async-start | bytes 6291456 | tf_op jit(solution)/shard_map/all_to_all | solution.py:141
  546.0 34.0 %copy-start.6 = (bf16[12,128,768]{1,2,0:T(8,128)(2,1)S(1)}, bf16[12,128,768]{1,2,0:T(8,128)(2,1)}, u32[]{:S(2)}) copy-start(bf16[12,128,768]{1,2,0:T(8,128)(2,1)} %copy-done.5) | copy-start | bytes 7077892
  575.5 42.4 %all-to-all-start.7 = ((bf16[12,128,768]{2,0,1:T(8,128)(2,1)}), bf16[12,128,768]{2,0,1:T(8,128)(2,1)}, u32[]{:S(2)}, u32[]{:S(2)}) async-start(bf16[12,128,768]{2,0,1:T(8,128)(2,1)} %copy.120), calls=%async_computation.7 | async-start | bytes 6291456 | tf_op jit(solution)/shard_map/all_to_all | solution.py:143
  617.9 41.5 %all-to-all-start.6 = ((bf16[12,128,768]{2,0,1:T(8,128)(2,1)}), bf16[12,128,768]{2,0,1:T(8,128)(2,1)S(1)}, u32[]{:S(2)}, u32[]{:S(2)}) async-start(bf16[12,128,768]{2,0,1:T(8,128)(2,1)} %copy.116), calls=%async_computation.6 | async-start | bytes 6291456 | tf_op jit(solution)/shard_map/all_to_all | solution.py:142
  621.5 145.5 %reduce-scatter.13.cloned.1.call-start = ((), (), s32[]{:S(2)}) async-start(), calls=%async_computation.19 | async-start | bytes 4423680
  662.5 10.0 slice-start.2
  686.7 96.6 %reduce-scatter.7.cloned.1.call-start = ((), (), s32[]{:S(2)}) async-start(), calls=%async_computation.16 | async-start | bytes 1474560 | tf_op jit(solution)/shard_map/reduce_scatter | solution.py:310
  693.4 176.2 %reduce-scatter.9.cloned.1.call-start = ((), (), s32[]{:S(2)}) async-start(), calls=%async_computation.17 | async-start | bytes 5898240 | tf_op jit(solution)/shard_map/reduce_scatter | solution.py:322
  707.6 250.2 %reduce-scatter.11.cloned.1.call-start = ((), (), s32[]{:S(2)}) async-start(), calls=%async_computation.18 | async-start | bytes 5898240 | tf_op jit(solution)/shard_map/reduce_scatter | solution.py:328
  720.9 42.2 %copy-start.23 = (f32[1536]{0:T(1024)S(1)}, f32[1536]{0:T(1024)}, u32[]{:S(2)}) copy-start(f32[1536]{0:T(1024)} %copy-done.22) | copy-start | bytes 18436
  720.9 42.2 %copy-start.25 = (f32[1536]{0:T(1024)S(1)}, f32[1536]{0:T(1024)}, u32[]{:S(2)}) copy-start(f32[1536]{0:T(1024)} %copy-done.24) | copy-start | bytes 18436
  720.9 42.2 %copy-start.28 = (f32[768]{0:T(1024)S(1)}, f32[768]{0:T(1024)}, u32[]{:S(2)}) copy-start(f32[768]{0:T(1024)} %copy-done.26) | copy-start | bytes 9220
  721.0 319.7 %all-reduce.23.cloned.1.call-start = ((), (), s32[]{:S(2)}) async-start(), calls=%async_computation.20 | async-start | bytes 7667712 | tf_op jit(solution)/shard_map/psum | solution.py:342
  767.0 190.8 %copy-start.48 = (bf16[768,2304]{1,0:T(8,128)(2,1)S(1)}, bf16[768,2304]{1,0:T(8,128)(2,1)}, u32[]{:S(2)}) copy-start(bf16[768,2304]{1,0:T(8,128)(2,1)} %all-gather.6.cloned.1.call-done) | copy-start | bytes 10616836
  (43 other events, 206.6 us)
Sparse Core Ops, SparseCore 0:
  9.6 72.8 all-gather.5
  119.6 29.6 all-gather.7
  162.0 88.5 all-gather.9
  265.2 88.6 all-gather.11
  686.8 64.2 reduce-scatter.12
  753.9 29.4 reduce-scatter.6
  785.7 83.9 reduce-scatter.8
  872.0 85.7 reduce-scatter.10
  962.1 78.5 all-reduce.22
where the time goes:
time: 1070 us; the launch traced here: 1060 us
  waiting for transfers between devices  463 us (43%)
  matrix products  263 us (25%)
  local copies, waits for them, and re-layouts  146 us (14%)
  blocking collectives  80.8 us (8%)
  other arithmetic  50.9 us (5%)
  starting transfers between devices  35.2 us (3%)
  between operations  17 us (2%)
    reduce_scatter x1, waiting for transfers between devices, per_device(): lax.psum_scatter(grad_reduce.astype(jnp.bfloat16), 'batch', scatter_dimen...  88.1 us
    reduce_scatter x1, waiting for transfers between devices, per_device(): lax.psum_scatter(grad_expand.astype(jnp.bfloat16), 'batch', scatter_dimen...  86.3 us
    psum x1, waiting for transfers between devices, per_device(): lax.psum(owned[0].astype(jnp.bfloat16), 'seq').astype(jnp.float32)  72.3 us
    dot_general x3, matrix products, make_step(): total = jnp.dot(left, pieces[0], preferred_element_type=jnp.float32)  67.3 us
    dot_general x4, matrix products, transpose_right(): lax.dot_general(first, second, (((1,), (1,)), ((), ())), preferred_elemen...  47 us
    unnamed x2, blocking collectives  41.9 us
    dot_general x4, matrix products, transpose_left(): lax.dot_general(first, second, (((0,), (0,)), ((), ())), preferred_elemen...  39.9 us
    all_to_all x1, waiting for transfers between devices, per_device(): lax.all_to_all(grad_sorted, 'seq', split_axis=1, concat_axis=1, tiled=True)  37.8 us
  transfers between devices with their start and end apart: 17, of which 13 were waited for; matrix products, arithmetic and copies ran while one was open for 26% of the time, Pallas kernels for 0%

commit v1 on v0

--- a/solution.py
+++ b/solution.py
@@ -1,8 +1,11 @@
+import functools
 import math
 
 import jax
 import jax.numpy as jnp
 from jax import lax
+from jax.experimental import pallas as pl
+from jax.experimental.pallas import tpu as pltpu
 from jax.sharding import PartitionSpec as P
 
 epsilon = 1e-05
@@ -372,6 +375,852 @@
     )
 
 
+MESH = pl.DeviceIdType.MESH
+f32 = jnp.float32
+bf16 = jnp.bfloat16
+
+
+class Place:
+    def __init__(self, chips, depth):
+        self.chips, self.depth = chips, depth
+        self.z = lax.axis_index("batch")
+        spot = lax.axis_index("seq")
+        self.chip, self.core = lax.div(spot, 2), lax.rem(spot, 2)
+
+    def chip_at(self, k):
+        return lax.rem(self.chip + k + self.chips, self.chips)
+
+    def z_at(self, k):
+        return lax.rem(self.z + k + self.depth, self.depth)
+
+    def plane(self, k):
+        return (self.z, self.chip_at(k) * 2 + self.core)
+
+    def tower(self, k):
+        return (self.z_at(k), self.chip * 2 + self.core)
+
+    def sibling(self):
+        return (self.z, self.chip * 2 + 1 - self.core)
+
+    def greet(self):
+        bell = pltpu.get_barrier_semaphore()
+        others = [self.plane(k) for k in range(1, self.chips)]
+        others += [self.tower(k) for k in range(1, self.depth)]
+        others.append(self.sibling())
+        for other in others:
+            pl.semaphore_signal(bell, inc=1, device_id=other, device_id_type=MESH)
+        pl.semaphore_wait(bell, len(others))
+
+
+def far_copy(src, dst, sems, at, device):
+    return pltpu.make_async_remote_copy(
+        src_ref=src,
+        dst_ref=dst,
+        send_sem=sems[0].at[at],
+        recv_sem=sems[1].at[at],
+        device_id=device,
+        device_id_type=MESH,
+    )
+
+
+def one_hot(row, slots):
+    return jnp.where(slots == row, 1.0, 0.0).astype(bf16)
+
+
+def split_lanes(tile, low):
+    zero = jnp.zeros_like(tile)
+    return jnp.where(low, tile, zero), jnp.where(low, zero, tile)
+
+
+def stack_lanes(tile, low):
+    first, second = split_lanes(tile, low)
+    return jnp.concatenate([first, second], axis=0)
+
+
+def dot_rows(a, b):
+    return jnp.dot(a, b, preferred_element_type=f32)
+
+
+def dot_lanes(a, b):
+    return lax.dot_general(a, b, (((1,), (1,)), ((), ())), preferred_element_type=f32)
+
+
+def dot_first(a, b):
+    return lax.dot_general(a, b, (((0,), (0,)), ((), ())), preferred_element_type=f32)
+
+
+def multiple(value, by):
+    return pl.multiple_of(value, by)
+
+
+def attend_kernel(
+    chips,
+    depth,
+    heads,
+    tok_ref,
+    pos_ref,
+    aw_ref,
+    vec_ref,
+    ow_ref,
+    ew_ref,
+    rw_ref,
+    x_out,
+    ctx_out,
+    q_out,
+    k_out,
+    v_out,
+    p_out,
+    pos_out,
+    aw_out,
+    vec_out,
+    ow_out,
+    ew_out,
+    rw_out,
+    xbuf,
+    posbuf,
+    wbuf,
+    vbuf,
+    bias,
+    qkv,
+    qs,
+    ks,
+    vs,
+    ps,
+    os,
+    ctxb,
+    tok_s,
+    tok_r,
+    tokc_s,
+    tokc_r,
+    pos_s,
+    pos_r,
+    posc_s,
+    posc_r,
+    aw_s,
+    aw_r,
+    awc_s,
+    awc_r,
+    vec_s,
+    vec_r,
+    wz_s,
+    wz_r,
+    wp_s,
+    wp_r,
+    wc_s,
+    wc_r,
+    ctx_s,
+    ctx_r,
+    loc,
+    out_sem,
+):
+    me = Place(chips, depth)
+    z, chip, core = me.z, me.chip, me.core
+    per = tok_ref.shape[0] // chips
+    half = aw_ref.shape[1] // 6
+    rows_z = aw_ref.shape[0]
+    pairs = heads // 4
+    size = half // (2 * pairs)
+    me.greet()
+
+    def aw_copy(k, part):
+        columns = pl.ds(multiple(part * 2 * half + core * half, 128), half)
+        return far_copy(
+            aw_ref.at[:, columns],
+            wbuf.at[pl.ds(multiple(z * rows_z, 8), rows_z), pl.ds(part * half, half)],
+            (aw_s, aw_r),
+            (k - 1) * 3 + part,
+            me.tower(k),
+        )
+
+    def mine(ref, target):
+        return ref.at[pl.ds(target * per, per)]
+
+    def tok_copy(k):
+        return far_copy(
+            mine(tok_ref, me.chip_at(k)), xbuf.at[core, chip], (tok_s, tok_r), k - 1, me.plane(k)
+        )
+
+    def pos_copy(k):
+        return far_copy(
+            mine(pos_ref, me.chip_at(k)), posbuf.at[core, chip], (pos_s, pos_r), k - 1, me.plane(k)
+        )
+
+    def vec_copy(k):
+        return far_copy(vec_ref, vbuf.at[z], (vec_s, vec_r), k - 1, me.tower(k))
+
+    sends = []
+    for k in range(1, chips):
+        sends.append(pos_copy(k))
+        sends[-1].start()
+    for k in range(1, depth):
+        sends.append(vec_copy(k))
+        sends[-1].start()
+    for k in range(1, max(chips, depth)):
+        if k < depth:
+            for part in range(3):
+                sends.append(aw_copy(k, part))
+                sends[-1].start()
+        if k < chips:
+            sends.append(tok_copy(k))
+            sends[-1].start()
+    local = []
+
+    def keep(src, dst):
+        copy = pltpu.make_async_copy(src, dst, loc.at[len(local)])
+        copy.start()
+        local.append(copy)
+
+    keep(mine(tok_ref, chip), xbuf.at[core, chip])
+    keep(mine(pos_ref, chip), posbuf.at[core, chip])
+    keep(vec_ref, vbuf.at[z])
+    for part in range(3):
+        keep(
+            aw_ref.at[:, pl.ds(multiple(part * 2 * half + core * half, 128), half)],
+            wbuf.at[pl.ds(multiple(z * rows_z, 8), rows_z), pl.ds(part * half, half)],
+        )
+    eighth = ow_ref.shape[0] // (2 * chips)
+    wide = ew_ref.shape[1] // (2 * chips)
+    tall = rw_ref.shape[0] // (2 * chips)
+
+    def piece(ref, kind, at):
+        if kind == 0:
+            return ref.at[pl.ds(multiple(at * eighth, 8), eighth)]
+        if kind == 1:
+            return ref.at[:, pl.ds(multiple(at * wide, 128), wide)]
+        return ref.at[pl.ds(multiple(at * tall, 8), tall)]
+
+    shards = (ow_ref, ew_ref, rw_ref)
+    fulls = (ow_out, ew_out, rw_out)
+    mine_at = core * chips + chip
+
+    def place(kind, zz, at):
+        if kind == 0:
+            return ow_out.at[zz, at]
+        if kind == 1:
+            return ew_out.at[zz, :, pl.ds(multiple(at * wide, 128), wide)]
+        return rw_out.at[zz, at]
+
+    def place_all(kind, at):
+        if kind == 0:
+            return ow_out.at[:, at]
+        if kind == 1:
+            return ew_out.at[:, :, pl.ds(multiple(at * wide, 128), wide)]
+        return rw_out.at[:, at]
+
+    for kind in range(3):
+        keep(piece(shards[kind], kind, mine_at), place(kind, z, mine_at))
+
+    def wz_copy(kind, k):
+        return far_copy(
+            piece(shards[kind], kind, mine_at),
+            place(kind, z, mine_at),
+            (wz_s, wz_r),
+            kind * (depth - 1) + k - 1,
+            me.tower(k),
+        )
+
+    def wp_copy(kind, k, origin):
+        at = core * chips + origin
+        return far_copy(
+            place_all(kind, at),
+            place_all(kind, at),
+            (wp_s, wp_r),
+            kind * (chips - 1) + k - 1,
+            me.plane(k),
+        )
+
+    def wc_copy(kind, origin_k):
+        at = core * chips + me.chip_at(origin_k)
+        return far_copy(
+            place_all(kind, at),
+            place_all(kind, at),
+            (wc_s, wc_r),
+            kind * chips + origin_k,
+            me.sibling(),
+        )
+
+    for copy in local[:2]:
+        copy.wait()
+
+    def tokc_copy(k):
+        source = me.chip_at(-k)
+        return far_copy(
+            xbuf.at[core, source], xbuf.at[core, source], (tokc_s, tokc_r), k, me.sibling()
+        )
+
+    def posc_copy(k):
+        source = me.chip_at(-k)
+        return far_copy(
+            posbuf.at[core, source], posbuf.at[core, source], (posc_s, posc_r), k, me.sibling()
+        )
+
+    for k in range(chips):
+        if k:
+            pos_copy(k).wait_recv()
+            tok_copy(k).wait_recv()
+        for copy in (posc_copy(k), tokc_copy(k)):
+            copy.start()
+            sends.append(copy)
+    for copy in local[2:6]:
+        copy.wait()
+    for k in range(1, depth):
+        vec_copy(k).wait_recv()
+        for part in range(3):
+            aw_copy(k, part).wait_recv()
+    for k in range(chips):
+        posc_copy(k).wait_recv()
+        tokc_copy(k).wait_recv()
+    for copy in local[6:]:
+        copy.wait()
+    for kind in range(3):
+        for k in range(1, depth):
+            sends.append(wz_copy(kind, k))
+            sends[-1].start()
+
+    outs = []
+
+    def emit(src, dst):
+        copy = pltpu.make_async_copy(src, dst, out_sem.at[len(outs)])
+        copy.start()
+        outs.append(copy)
+
+    emit(xbuf, x_out)
+    emit(posbuf, pos_out)
+    emit(wbuf, aw_out.at[core])
+    emit(vbuf, vec_out)
+    awc = far_copy(wbuf, aw_out.at[core], (awc_s, awc_r), 0, me.sibling())
+    awc.start()
+    sends.append(awc)
+
+    quarter = rows_z
+    for zz in range(depth):
+        begin = zz * quarter
+        for row, at in ((0, 0), (1, 2)):
+            for side in range(2):
+                lo = max(begin, side * half)
+                hi = min(begin + quarter, (side + 1) * half)
+                if lo < hi:
+                    bias[side, 0:1, at * half + lo - side * half : at * half + hi - side * half] = (
+                        vbuf[zz, row : row + 1, lo - begin : hi - begin]
+                    )
+    bias[0, 0:1, half : 2 * half] = jnp.zeros((1, half), f32)
+    bias[1, 0:1, half : 2 * half] = jnp.zeros((1, half), f32)
+    added = bias[core, 0:1, :]
+
+    cluster = tok_ref.shape[1]
+    blocks = 2 * chips
+    share = cluster // blocks
+    width = tok_ref.shape[2]
+
+    @pl.loop(0, blocks)
+    def _(jj):
+        x = xbuf[lax.div(jj, chips), lax.rem(jj, chips)].reshape(per * cluster, width)
+        mixed = (dot_rows(x, wbuf[...]) + added).astype(bf16)
+        for at in range(3 * pairs):
+            qkv[at, jj] = mixed[:, at * 128 : (at + 1) * 128].reshape(per, cluster, 128)
+
+    slots = lax.broadcasted_iota(jnp.int32, (cluster, cluster), 0)
+    low = lax.broadcasted_iota(jnp.int32, (cluster, 128), 1) < size
+    scale = size ** (-0.5)
+
+    def tables(jj, i, pair, part):
+        first = part * heads + core * (heads // 2) + 2 * pair
+        rows = [
+            one_hot(posbuf[jj // chips, jj % chips, i, pl.ds(first + h, 1), :], slots)
+            for h in range(2)
+        ]
+        return rows
+
+    def weights_step(stage):
+        if stage == 0:
+            for kind in range(3):
+                for k in range(1, depth):
+                    wz_copy(kind, k).wait_recv()
+                for k in range(1, chips):
+                    wp_copy(kind, k, chip).start()
+                wc_copy(kind, 0).start()
+
+    @pl.loop(0, per)
+    def _(i):
+        @pl.loop(0, pairs)
+        def _(pair):
+            at = i * pairs + pair
+            for jj in range(blocks):
+                tq = jnp.concatenate(tables(jj, i, pair, 0), axis=1)
+                tk = jnp.concatenate(tables(jj, i, pair, 1), axis=1)
+                q = stack_lanes(qkv[pair, jj, i], low)
+                k = stack_lanes(qkv[pairs + pair, jj, i], low)
+                v = stack_lanes(qkv[2 * pairs + pair, jj, i], low)
+                span = slice(jj * share, (jj + 1) * share)
+                sq = dot_rows(tq, q).astype(bf16)
+                skv = dot_rows(tk, jnp.concatenate([k, v], axis=1)).astype(bf16)
+                qs[at, :, span, :] = sq.reshape(blocks, share, 128)
+                ks[at, :, span, :] = skv[:, :128].reshape(blocks, share, 128)
+                vs[at, :, span, :] = skv[:, 128:].reshape(blocks, share, 128)
+            for c in range(blocks):
+                scores = dot_lanes(qs[at, c], stack_lanes(ks[at, c], low)) * scale
+                halves = []
+                for h in range(2):
+                    s = scores[:, h * cluster : (h + 1) * cluster]
+                    e = jnp.exp(s - jnp.max(s, axis=1, keepdims=True))
+                    halves.append((e / jnp.sum(e, axis=1, keepdims=True)).astype(bf16))
+                probs = jnp.concatenate(halves, axis=1)
+                ps[at, c] = probs
+                o = dot_rows(probs, stack_lanes(vs[at, c], low)).astype(bf16)
+                os[c] = o
+            for jj in range(blocks):
+                tq = jnp.concatenate(tables(jj, i, pair, 0), axis=0)
+                rows = os[:, jj * share : (jj + 1) * share, :].reshape(cluster, 128)
+                back = dot_first(tq, stack_lanes(rows, low)).astype(bf16)
+                ctxb[jj // chips, jj % chips, i, :, pl.ds(multiple(pair * 128, 128), 128)] = back
+
+        @pl.when(i == 0)
+        def _():
+            weights_step(0)
+
+    far = far_copy(
+        ctxb.at[1 - core],
+        ctx_out.at[:, :, :, pl.ds(multiple(core * half, 128), half)],
+        (ctx_s, ctx_r),
+        0,
+        me.sibling(),
+    )
+    far.start()
+    emit(ctxb.at[core], ctx_out.at[:, :, :, pl.ds(multiple(core * half, 128), half)])
+    emit(qs, q_out)
+    emit(ks, k_out)
+    emit(vs, v_out)
+    emit(ps, p_out)
+    for kind in range(3):
+        for k in range(1, chips):
+            wp_copy(kind, k, me.chip_at(-k)).wait_recv()
+            wc_copy(kind, chips - k).start()
+    for kind in range(3):
+        for k in range(chips):
+            wc_copy(kind, k).wait()
+        for k in range(1, chips):
+            wp_copy(kind, k, chip).wait_send()
+    far.wait()
+    awc.wait_recv()
+    for copy in sends:
+        copy.wait_send()
+    for copy in outs:
+        copy.wait()
+
+
+def attend(tokens, pos, attend_weight, vectors, output_weight, expand_weight, reduce_weight, chips, depth, heads):
+    seqs, cluster, width = tokens.shape
+    per, blocks, pairs = seqs // chips, 2 * chips, heads // 4
+    half = width // 2
+    rows_z = attend_weight.shape[0]
+    wide = expand_weight.shape[1]
+    items = per * pairs
+    dma = pltpu.SemaphoreType.DMA
+    anywhere = pl.BlockSpec(memory_space=pl.ANY)
+    eighth = output_weight.shape[0] // blocks
+    tall = reduce_weight.shape[0] // blocks
+    shapes = [
+        ((2, chips, per, cluster, width), bf16),
+        ((chips, per, cluster, width), bf16),
+        ((items, blocks, cluster, 128), bf16),
+        ((items, blocks, cluster, 128), bf16),
+        ((items, blocks, cluster, 128), bf16),
+        ((items, blocks, cluster, 2 * cluster), bf16),
+        ((2, chips, per, 2 * heads, cluster), jnp.int32),
+        ((2, depth * rows_z, 3 * half), bf16),
+        ((depth,) + vectors.shape, f32),
+        ((depth, blocks, eighth, width), bf16),
+        ((depth, rows_z, wide), bf16),
+        ((depth, blocks, tall, width), bf16),
+    ]
+    t, c = depth - 1, chips - 1
+    return pl.pallas_call(
+        functools.partial(attend_kernel, chips, depth, heads),
+        out_shape=[jax.ShapeDtypeStruct(*s) for s in shapes],
+        in_specs=[anywhere] * 7,
+        out_specs=[anywhere] * len(shapes),
+        scratch_shapes=[
+            pltpu.VMEM(shapes[0][0], bf16),
+            pltpu.VMEM(shapes[6][0], jnp.int32),
+            pltpu.VMEM(shapes[7][0][1:], bf16),
+            pltpu.VMEM(shapes[8][0], f32),
+            pltpu.VMEM((2, 8, 3 * half), f32),
+            pltpu.VMEM((3 * pairs, blocks, per, cluster, 128), bf16),
+            pltpu.VMEM(shapes[2][0], bf16),
+            pltpu.VMEM(shapes[3][0], bf16),
+            pltpu.VMEM(shapes[4][0], bf16),
+            pltpu.VMEM(shapes[5][0], bf16),
+            pltpu.VMEM((blocks, cluster, 128), bf16),
+            pltpu.VMEM((2, chips, per, cluster, half), bf16),
+            dma((c,)), dma((c,)), dma((chips,)), dma((chips,)),
+            dma((c,)), dma((c,)), dma((chips,)), dma((chips,)),
+            dma((3 * t,)), dma((3 * t,)), dma((1,)), dma((1,)),
+            dma((t,)), dma((t,)),
+            dma((3 * t,)), dma((3 * t,)),
+            dma((3 * c,)), dma((3 * c,)),
+            dma((3 * chips,)), dma((3 * chips,)),
+            dma((1,)), dma((1,)),
+            dma((9,)), dma((9,)),
+        ],
+        compiler_params=pltpu.CompilerParams(
+            collective_id=1, has_side_effects=True, vmem_limit_bytes=60 * 2**20
+        ),
+        name="attend",
+    )(tokens, pos, attend_weight, vectors, output_weight, expand_weight, reduce_weight)
+
+
+def attend_back_kernel(
+    chips,
+    depth,
+    heads,
+    d_ref,
+    q_ref,
+    k_ref,
+    v_ref,
+    p_ref,
+    pos_ref,
+    x_ref,
+    g_out,
+    dw_out,
+    db_out,
+    dbuf,
+    qs,
+    ks,
+    vs,
+    ps,
+    posbuf,
+    xbuf,
+    ds,
+    gs,
+    gbuf,
+    dw,
+    db,
+    d_s,
+    d_r,
+    g_s,
+    g_r,
+    loc,
+):
+    me = Place(chips, depth)
+    core = me.core
+    per = d_ref.shape[1]
+    cluster, width = d_ref.shape[2], d_ref.shape[3]
+    half = width // 2
+    pairs = heads // 4
+    size = half // (2 * pairs)
+    blocks = 2 * chips
+    share = cluster // blocks
+    me.greet()
+    theirs = pl.ds(multiple((1 - core) * half, 128), half)
+    far = far_copy(d_ref.at[:, :, :, theirs], dbuf.at[core], (d_s, d_r), 0, me.sibling())
+    far.start()
+    local = []
+
+    def keep(src, dst):
+        copy = pltpu.make_async_copy(src, dst, loc.at[len(local)])
+        copy.start()
+        local.append(copy)
+
+    keep(d_ref.at[:, :, :, pl.ds(multiple(core * half, 128), half)], dbuf.at[core])
+    keep(pos_ref, posbuf)
+    keep(q_ref, qs)
+    keep(k_ref, ks)
+    keep(v_ref, vs)
+    keep(p_ref, ps)
+    keep(x_ref, xbuf)
+    for copy in local[:6]:
+        copy.wait()
+    far.wait()
+    slots = lax.broadcasted_iota(jnp.int32, (cluster, cluster), 0)
+    low = lax.broadcasted_iota(jnp.int32, (cluster, 128), 1) < size
+    scale = size ** (-0.5)
+    db[...] = jnp.zeros_like(db)
+    dw[...] = jnp.zeros_like(dw)
+
+    def tables(jj, i, pair, part):
+        first = part * heads + core * (heads // 2) + 2 * pair
+        return [
+            one_hot(posbuf[jj // chips, jj % chips, i, pl.ds(first + h, 1), :], slots)
+            for h in range(2)
+        ]
+
+    for copy in local[6:]:
+        copy.wait()
+
+    @pl.loop(0, per)
+    def _(i):
+        @pl.loop(0, pairs)
+        def _(pair):
+            at = i * pairs + pair
+            lanes = pl.ds(multiple(pair * 128, 128), 128)
+            for jj in range(blocks):
+                tq = jnp.concatenate(tables(jj, i, pair, 0), axis=1)
+                rows = stack_lanes(dbuf[jj // chips, jj % chips, i, :, lanes], low)
+                ds[:, jj * share : (jj + 1) * share, :] = (
+                    dot_rows(tq, rows).astype(bf16).reshape(blocks, share, 128)
+                )
+            for c in range(blocks):
+                d = ds[c]
+                probs = ps[at, c]
+                slope = dot_lanes(d, stack_lanes(vs[at, c], low))
+                wide = probs.astype(f32)
+                halves = []
+                for h in range(2):
+                    span = slice(h * cluster, (h + 1) * cluster)
+                    inner = jnp.sum(wide[:, span] * slope[:, span], axis=1, keepdims=True)
+                    halves.append((wide[:, span] * (slope[:, span] - inner)).astype(bf16))
+                grads = jnp.concatenate(halves, axis=1)
+                gq = dot_rows(grads, stack_lanes(ks[at, c], low)) * scale
+                gk = dot_first(grads, qs[at, c]) * scale
+                gv = dot_first(probs, d)
+                gs[0, c] = gq.astype(bf16)
+                gs[1, c] = jnp.where(low, gk[:cluster], gk[cluster:]).astype(bf16)
+                gs[2, c] = jnp.where(low, gv[:cluster], gv[cluster:]).astype(bf16)
+            for jj in range(blocks):
+                for part in range(3):
+                    if part < 2:
+                        table = jnp.concatenate(tables(jj, i, pair, part), axis=0)
+                    rows = gs[part, :, jj * share : (jj + 1) * share, :].reshape(cluster, 128)
+                    back = dot_first(table, stack_lanes(rows, low))
+                    to = pl.ds(multiple(part * half + pair * 128, 128), 128)
+                    gbuf[jj // chips, jj % chips, i, :, to] = back.astype(bf16)
+
+        for b in range(2):
+            x = jnp.concatenate([xbuf[b, j, i] for j in range(chips)], axis=0)
+            g = jnp.concatenate([gbuf[b, j, i] for j in range(chips)], axis=0)
+            dw[...] += dot_first(x, g)
+            db[0:1, :] += jnp.sum(g.astype(f32), axis=0, keepdims=True)
+
+    give = far_copy(gbuf.at[1 - core], g_out.at[core], (g_s, g_r), 0, me.sibling())
+    give.start()
+    tail = []
+    for n, (src, dst) in enumerate(
+        ((gbuf.at[core], g_out.at[core]), (dw, dw_out), (db, db_out))
+    ):
+        tail.append(pltpu.make_async_copy(src, dst, loc.at[n]))
+        tail[-1].start()
+    for copy in tail:
+        copy.wait()
+    give.wait()
+
+
+def attend_back(grad_context, q, k, v, p, pos, x, depth, heads):
+    chips, per, cluster, width = grad_context.shape
+    half, blocks, pairs = width // 2, 2 * chips, heads // 4
+    dma = pltpu.SemaphoreType.DMA
+    anywhere = pl.BlockSpec(memory_space=pl.ANY)
+    shapes = [
+        ((2, chips, per, cluster, 3 * half), bf16),
+        ((width, 3 * half), f32),
+        ((8, 3 * half), f32),
+    ]
+    return pl.pallas_call(
+        functools.partial(attend_back_kernel, chips, depth, heads),
+        out_shape=[jax.ShapeDtypeStruct(*s) for s in shapes],
+        in_specs=[anywhere] * 7,
+        out_specs=[anywhere] * 3,
+        scratch_shapes=[
+            pltpu.VMEM((2, chips, per, cluster, half), bf16),
+            pltpu.VMEM(q.shape, bf16),
+            pltpu.VMEM(q.shape, bf16),
+            pltpu.VMEM(q.shape, bf16),
+            pltpu.VMEM(p.shape, bf16),
+            pltpu.VMEM(pos.shape, jnp.int32),
+            pltpu.VMEM(x.shape, bf16),
+            pltpu.VMEM((blocks, cluster, 128), bf16),
+            pltpu.VMEM((3, blocks, cluster, 128), bf16),
+            pltpu.VMEM(shapes[0][0], bf16),
+            pltpu.VMEM(shapes[1][0], f32),
+            pltpu.VMEM(shapes[2][0], f32),
+            dma((1,)), dma((1,)), dma((1,)), dma((1,)),
+            dma((7,)),
+        ],
+        compiler_params=pltpu.CompilerParams(
+            collective_id=2, has_side_effects=True, vmem_limit_bytes=60 * 2**20
+        ),
+        name="attend_back",
+    )(grad_context, q, k, v, p, pos, x)
+
+
+def places(rank, cluster, share):
+    seqs, rows, length = rank.shape
+    clusters = cluster // share
+    target = rank // cluster
+    which = lax.broadcasted_iota(jnp.int32, (1, 1, clusters, 1), 2)
+    inside = (target[:, :, None, :] == which).astype(bf16)
+    first = lax.broadcasted_iota(jnp.int32, (length, length), 0)
+    second = lax.broadcasted_iota(jnp.int32, (length, length), 1)
+    before = (first < second).astype(bf16)
+    count = lax.dot_general(
+        inside.reshape(seqs * rows * clusters, length),
+        before,
+        (((1,), (0,)), ((), ())),
+        preferred_element_type=f32,
+    ).reshape(seqs, rows, clusters, length)
+    spot = which.astype(f32) * share + count
+    return jnp.sum(inside.astype(f32) * spot, axis=2).astype(jnp.int32)
+
+
+def per_chip(
+    tokens,
+    attend_weight,
+    query_bias,
+    value_bias,
+    output_weight,
+    output_bias,
+    first_gain,
+    first_shift,
+    expand_weight,
+    expand_bias,
+    reduce_weight,
+    reduce_bias,
+    second_gain,
+    second_shift,
+    query_rank,
+    key_rank,
+    cotangent,
+):
+    seqs, cluster, width = tokens.shape
+    heads = query_rank.shape[1]
+    owners = lax.axis_size("seq")
+    depth = lax.axis_size("batch")
+    chips = owners // 2
+    per = seqs // chips
+    rows = seqs * cluster
+    half = width // 2
+    share = cluster // owners
+    core = lax.rem(lax.axis_index("seq"), 2)
+    groups = [[2 * p + c for p in range(chips)] for c in range(2)]
+
+    def swap(x):
+        return lax.all_to_all(
+            x, "seq", split_axis=0, concat_axis=0, tiled=True, axis_index_groups=groups
+        )
+
+    pos = places(jnp.concatenate([query_rank, key_rank], axis=1), cluster, share)
+    quarter = width // depth
+    small = jnp.concatenate(
+        [
+            v.astype(f32)
+            for v in (
+                query_bias,
+                value_bias,
+                output_bias,
+                first_gain,
+                first_shift,
+                reduce_bias,
+                second_gain,
+                second_shift,
+                expand_bias,
+            )
+        ]
+    )
+    count = small.shape[0] // quarter
+    vectors = jnp.pad(small.reshape(count, quarter), ((0, 16 - count), (0, 256 - quarter)))
+    (x_all, context, qs, ks, vs, ps, pos_all, attend_all, vec_all, out_all, exp_all, red_all) = attend(
+        tokens, pos, attend_weight, vectors, output_weight, expand_weight, reduce_weight, chips, depth, heads
+    )
+    full = jnp.transpose(vec_all[:, :8, :quarter], (1, 0, 2)).reshape(8, width)
+    bias_up = vec_all[:, 8:count, :quarter].reshape(-1)
+    output_full = out_all.reshape(width, width)
+    expand_full = exp_all.reshape(width, -1)
+    reduce_full = red_all.reshape(-1, width)
+    mine = lax.dynamic_index_in_dim(x_all, core, 0, keepdims=False).reshape(rows, width)
+    context = context.reshape(rows, width)
+    resid_one = mine.astype(f32) + jnp.dot(context, output_full, preferred_element_type=f32) + full[2]
+    middle, normed_one, inverse_one = layer_norm(resid_one, full[3], full[4])
+    middle_low = lax.optimization_barrier(middle.astype(bf16))
+    pre = jnp.dot(middle_low, expand_full, preferred_element_type=f32) + bias_up
+    hidden = jax.nn.gelu(pre, approximate=False).astype(bf16)
+    hidden = lax.optimization_barrier(hidden)
+    resid_two = middle + jnp.dot(hidden, reduce_full, preferred_element_type=f32) + full[5]
+    final, normed_two, inverse_two = layer_norm(resid_two, full[6], full[7])
+    layer_out = swap(final.astype(bf16).reshape(seqs, cluster, width))
+    upstream = swap(cotangent).reshape(rows, width).astype(f32)
+    grad_second_gain = jnp.sum(upstream * normed_two, axis=0)
+    grad_second_shift = jnp.sum(upstream, axis=0)
+    grad_resid_two = norm_back(upstream, normed_two, inverse_two, full[6])
+    grad_branch_two = grad_resid_two.astype(bf16)
+    grad_reduce_bias = jnp.sum(grad_branch_two, axis=0, dtype=f32)
+    grad_reduce = transpose_left(hidden, grad_branch_two)
+    grad_hidden = transpose_right(grad_branch_two, reduce_full)
+    grad_pre = (grad_hidden * gelu_slope(pre)).astype(bf16)
+    grad_pre = lax.optimization_barrier(grad_pre)
+    grad_expand_bias = jnp.sum(grad_pre, axis=0, dtype=f32)
+    grad_expand = transpose_left(middle_low, grad_pre)
+    grad_middle = grad_resid_two + transpose_right(grad_pre, expand_full)
+    grad_first_gain = jnp.sum(grad_middle * normed_one, axis=0)
+    grad_first_shift = jnp.sum(grad_middle, axis=0)
+    grad_resid_one = norm_back(grad_middle, normed_one, inverse_one, full[3])
+    grad_branch_one = grad_resid_one.astype(bf16)
+    grad_output_bias = jnp.sum(grad_branch_one, axis=0, dtype=f32)
+    grad_output = transpose_left(context, grad_branch_one)
+    grad_context = transpose_right(grad_branch_one, output_full).astype(bf16)
+    grads, grad_attend_half, grad_bias_half = attend_back(
+        grad_context.reshape(chips, per, cluster, width), qs, ks, vs, ps, pos_all, x_all, depth, heads
+    )
+    grads = grads.reshape(2, rows, 3 * half)
+    token_grad = grad_resid_one
+    for c in range(2):
+        token_grad = token_grad + transpose_right(grads[c], attend_all[c])
+    token_grad = swap(token_grad.astype(bf16).reshape(seqs, cluster, width))
+
+    def spread(part):
+        zero = jnp.zeros_like(part)
+        pick = core == 0
+        return jnp.where(pick, part, zero), jnp.where(pick, zero, part)
+
+    columns = []
+    for part in range(3):
+        columns += spread(grad_attend_half[:, part * half : (part + 1) * half])
+    grad_attend = jnp.concatenate(columns, axis=1)
+    grad_query_bias = jnp.concatenate(spread(grad_bias_half[0, :half]))
+    grad_value_bias = jnp.concatenate(spread(grad_bias_half[0, 2 * half :]))
+
+    def owned(grad):
+        part = lax.psum_scatter(grad.astype(bf16), "batch", scatter_dimension=0, tiled=True)
+        return lax.psum(part, "seq").astype(f32)
+
+    return (
+        layer_out,
+        token_grad,
+        owned(grad_attend),
+        owned(grad_query_bias),
+        owned(grad_value_bias),
+        owned(grad_output),
+        owned(grad_output_bias),
+        owned(grad_first_gain),
+        owned(grad_first_shift),
+        owned(grad_expand),
+        owned(grad_expand_bias),
+        owned(grad_reduce),
+        owned(grad_reduce_bias),
+        owned(grad_second_gain),
+        owned(grad_second_shift),
+    )
+
+
+def layer(mesh):
+    def run(*arrays):
+        seqs, cluster, width = arrays[0].shape
+        heads = arrays[14].shape[1]
+        owners, depth = mesh.shape["seq"], mesh.shape["batch"]
+        chips = owners // 2
+        fits = (
+            owners % 2 == 0
+            and chips > 1
+            and depth > 1
+            and seqs % chips == 0
+            and cluster == 128
+            and heads % 4 == 0
+            and width == heads * 64
+            and cluster % (16 * owners) == 0
+        )
+        return (per_chip if fits else per_device)(*arrays)
+
+    return run
+
+
 def solution(mesh):
     in_specs = (
         P("batch", "seq", None),
@@ -410,5 +1259,5 @@
         P("batch"),
     )
     return jax.shard_map(
-        per_device, mesh=mesh, in_specs=in_specs, out_specs=out_specs, check_vma=False
-    )
+        layer(mesh), mesh=mesh, in_specs=in_specs, out_specs=out_specs, check_vma=False
+    )

time: 1070 us -> 706 us (0.66)
  waiting for transfers between devices: 463 us -> 197 us
  Pallas kernels: 0 us -> 188 us
  matrix products: 263 us -> 142 us
  local copies, waits for them, and re-layouts: 146 us -> 25.3 us
  starting transfers between devices: 35.2 us -> 10.4 us
  blocking collectives: 80.8 us -> 62.8 us
    pallas_call x0 -> x2, Pallas kernels: none -> 188 us  [the longest x1 130 us: attend(): pl.pallas_call(functools.partial(attend_kernel, chips, depth, heads), out...]
    all_to_all x8 -> x2, waiting for transfers between devices: 163 us -> 0.01 us  [swap(): lax.all_to_all(x, 'seq', split_axis=0, concat_axis=0, tiled=True, axis_in...]
    dot_general x18 -> x4, matrix products: 176 us -> 66.8 us  [the longest x1 49.2 us: per_chip(): pre = jnp.dot(middle_low, expand_full, preferred_element_type=f32) + bias_up]
    psum x1, waiting for transfers between devices: 72.3 us -> 32.1 us  [owned(): return lax.psum(part, 'seq').astype(f32)]
    all_gather x4 -> x0, waiting for transfers between devices: 36.8 us -> none  [the longest x1 36.7 us: per_device(): lax.all_gather(attend_weight, 'batch', axis=0, tiled=True)]
    all_to_all x8 -> x0, local copies, waits for them, and re-layouts: 32.5 us -> none  [the longest x1 4.79 us: send_grads(): lax.all_to_all(grads[0], 'seq', split_axis=1, concat_axis=1, tiled=True)]
    all_to_all x0 -> x1, blocking collectives: none -> 32.3 us  [swap(): lax.all_to_all(x, 'seq', split_axis=0, concat_axis=0, tiled=True, axis_in...]
    another operation x4 -> x0, local copies, waits for them, and re-layouts: 28.3 us -> none  [sort_heads(): split = rows.reshape(seqs, length, heads, width // heads)]
  transfers between devices with their start and end apart: 17 -> 7, of which waited for: 13 -> 3; matrix products, arithmetic and copies ran while one was open for 26% -> 21% of each run, Pallas kernels for 0% -> 27%
where the time goes in v1:
time: 706 us; the launch traced here: 696 us
  waiting for transfers between devices  197 us (28%)
  Pallas kernels  188 us (27%)
  matrix products  142 us (20%)
  blocking collectives  62.8 us (9%)
  other arithmetic  55.1 us (8%)
  local copies, waits for them, and re-layouts  25.3 us (4%)
  between operations  16 us (2%)
  starting transfers between devices  10.4 us (1%)
    reduce_scatter x4, waiting for transfers between devices, owned(): lax.psum_scatter(grad.astype(bf16), 'batch', scatter_dimension=0, tiled=T...  165 us
    pallas_call x1, Pallas kernels, attend(): pl.pallas_call(functools.partial(attend_kernel, chips, depth, heads), out...  130 us
    pallas_call x1, Pallas kernels, attend_back(): pl.pallas_call(functools.partial(attend_back_kernel, chips, depth, heads)...  57.9 us
    dot_general x1, matrix products, per_chip(): pre = jnp.dot(middle_low, expand_full, preferred_element_type=f32) + bias_up  49.2 us
    dot_general x5, matrix products, transpose_right(): lax.dot_general(first, second, (((1,), (1,)), ((), ())), preferred_elemen...  45.6 us
    all_to_all x1, blocking collectives, swap(): lax.all_to_all(x, 'seq', split_axis=0, concat_axis=0, tiled=True, axis_in...  32.3 us
    psum x1, waiting for transfers between devices, owned(): return lax.psum(part, 'seq').astype(f32)  32.1 us
    dot_general x3, matrix products, transpose_left(): lax.dot_general(first, second, (((0,), (0,)), ((), ())), preferred_elemen...  29.3 us
  transfers between devices with their start and end apart: 7, of which 3 were waited for; matrix products, arithmetic and copies ran while one was open for 21% of the time, Pallas kernels for 27%

profile of v1, /device:TPU:0, one launch (start us, length us, event | category | flops | bytes accessed | tf_op | source)
XLA Modules:
  0.0 696.5 jit_solution(9042114433418441891)
XLA Ops:
  7.3 5.3 all-to-all-start.1
  14.9 129.6 %attend.1 = (bf16[2,4,3,128,768]{4,3,2,1,0:T(8,128)(2,1)}, bf16[4,3,128,768]{3,2,1,0:T(8,128)(2,1)}, bf16[9,8,128,128]{3,2,1,0:T(8,128)(2,1)}, bf16[9,8,128,128]...) custom-call(bf16[12,128,768]{2,1,0:T(8,128)(2,1)} %tok_ref.1, ...), custom_call_target="tpu_custom_call" | custom-call | tf_op jit(solution)/shard_map/attend/pallas_call | solution.py:837
  149.3 2.3 fusion.58
  154.6 2.9 fusion.24
  157.6 49.2 %fusion.2 = (bf16[1536,3072]{1,0:T(8,128)(2,1)}, f32[1536,3072]{1,0:T(8,128)}) fusion(f32[3072]{0:T(1024)S(1)} %add.169, bf16[1536,768]{1,0:T(8,128)(2,1)S(1)} %fusion.24, bf16[768,3072]{1,0:T(8,128)(2,1)} %bitcast.69), kind=kOutput, calls=%fused_computation.4 | convolution fusion | flops 7559184384 | bytes 35401728 | tf_op jit(solution)/shard_map/dot_general | solution.py:1133
  207.0 14.7 %fusion.59 = (f32[1536]{0:T(1024)S(1)}, f32[1536,768]{1,0:T(8,128)}) fusion(f32[768]{0:T(1024)S(1)} %add.173, bf16[1536,3072]{1,0:T(8,128)(2,1)} %get-tuple-element.92, bf16[3072,768]{1,0:T(8,128)(2,1)} %bitcast.71, f32[768]{0:T(1024)} %copy-done.17, f32[768]{0:T(1024)} %copy-done.15, f32[1536]{0:T(1024)} %copy-done.13, f32[1536,768]{1,0:T(8,128)} %copy-done, ...), kind=kOutput, calls=%fused_computation.129 | convolution fusion | flops 7256013312 | bytes 23620608 | tf_op jit(solution)/shard_map/dot_general | solution.py:1136
  221.8 3.0 multiply_reduce_fusion.2
  224.8 5.4 fusion.23
  230.3 2.3 fusion.22
  232.6 5.0 convert_reduce_fusion.1
  239.8 15.5 %fusion.8 = bf16[1536,3072]{1,0:T(8,128)(2,1)S(1)} fusion(f32[1536,3072]{1,0:T(8,128)} %get-tuple-element.93, bf16[3072,768]{1,0:T(8,128)(2,1)S(1)} %bitcast.74, f32[3072]{0:T(1024)S(1)} %add.169, f32[1536,768]{1,0:T(8,128)S(1)} %get-tuple-element.84), kind=kOutput, calls=%fused_computation.10 | convolution fusion | flops 7300841472 | bytes 37761024 | tf_op jit(solution)/shard_map/dot_general | solution.py:43
  255.4 17.6 %multiply_reduce_fusion = (bf16[768]{0:T(1024)(128)(2,1)S(1)}, f32[1536]{0:T(1024)S(1)}, f32[1536]{0:T(1024)S(1)}, bf16[768]{0:T(1024)(128)(2,1)}, f32[1536,768]{1,0:T(8,128)}) fusion(f32[1536,768]{1,0:T(8,128)S(1)} %bitcast.60, f32[1536]{0:T(1024)S(1)} %copy-done.14, f32[1536]{0:T(1024)S(1)} %copy-done.10, f32[768]{0:T(1024)S(1)} %copy-done.16, ...), kind=kOutput, calls=%fused_computation.40 | convolution fusion | flops 7259548672 | bytes 28342272 | tf_op jit(solution)/shard_map/dot_general | solution.py:43
  272.9 4.5 convert_reduce_fusion
  279.6 3.1 convolution_convert_fusion.3
  282.8 5.8 convolution_convert_fusion.2
  288.6 57.9 %attend_back.1 = (bf16[2,4,3,128,1152]{4,3,2,1,0:T(8,128)(2,1)}, f32[768,1152]{1,0:T(8,128)}, f32[8,1152]{1,0:T(8,128)}) custom-call(bf16[4,3,128,768]{3,2,1,0:T(8,128)(2,1)} %bitcast.66, bf16[9,8,128,128]{3,2,1,0:T(8,128)(2,1)} %get-tuple-element.36.q_ref, bf16[9,8,128,128]{3,2,1,0:T(8,128)(2,1)} %get-tuple-element.37.k_ref, ...), custom_call_target="tpu_custom_call" | custom-call | tf_op jit(solution)/shard_map/attend_back/pallas_call | solution.py:1017
  356.8 13.2 %convolution_convert_fusion = bf16[3072,768]{1,0:T(8,128)(2,1)} fusion(bf16[1536,3072]{1,0:T(8,128)(2,1)} %get-tuple-element.92, f32[1536,768]{1,0:T(8,128)} %copy-done.3), kind=kOutput, calls=%fused_computation.26 | convolution fusion | flops 7251296256 | bytes 18874368 | tf_op jit(solution)/shard_map/dot_general | solution.py:37
  371.8 12.9 %convolution_convert_fusion.1 = bf16[768,3072]{1,0:T(8,128)(2,1)} fusion(bf16[1536,768]{1,0:T(8,128)(2,1)S(1)} %copy-done.6, bf16[1536,3072]{1,0:T(8,128)(2,1)} %copy-done.1), kind=kOutput, calls=%fused_computation.27 | convolution fusion | flops 7250116608 | bytes 16515072 | tf_op jit(solution)/shard_map/dot_general | solution.py:37
  384.7 3.9 fusion.57
  388.9 3.3 fusion.26
  392.2 3.5 add_convert_fusion
  395.7 32.3 %all_to_all.15 = bf16[12,128,768]{2,1,0:T(8,128)(2,1)S(1)} all-to-all(bf16[12,128,768]{2,1,0:T(8,128)(2,1)S(1)} %bitcast.68), channel_id=1, replica_groups={{0,2,4,6},{1,3,5,7},{8,10,12,14},{9,11,13,15},{16,18,20,22},{17,19,21,2..., dimensions={0} | all-to-all | bytes 4718592 | tf_op jit(solution)/shard_map/all_to_all | solution.py:1096
  428.0 4.7 all-to-all-start
  433.1 77.3 %reduce-scatter.11.cloned.1.call-done = bf16[768,768]{1,0:T(8,128)(2,1)} async-done(((bf16[3072,768]{1,0:T(8,128)(2,1)}), bf16[768,768]{1,0:T(8,128)(2,1)}) %reduce-scatter.11.cloned.1.call-update) | async-done | bytes 1179664 | tf_op jit(solution)/shard_map/reduce_scatter | solution.py:1181
  510.3 88.0 %reduce-scatter.9.cloned.1.call-done = bf16[192,3072]{1,0:T(8,128)(2,1)} async-done(((bf16[768,3072]{1,0:T(8,128)(2,1)}), bf16[192,3072]{1,0:T(8,128)(2,1)}) %reduce-scatter.9.cloned.1.call-update) | async-done | bytes 1179664 | tf_op jit(solution)/shard_map/reduce_scatter | solution.py:1181
  600.3 5.5 reduce_sum.168
  608.6 18.2 %all-reduce.12 = (bf16[768]{0:T(1024)(128)(2,1)S(1)}, bf16[768]{0:T(1024)(128)(2,1)S(1)}, bf16[768]{0:T(1024)(128)(2,1)S(1)}, bf16[768]{0:T(1024)(128)(2,1)S(1)}...) all-reduce(bf16[768]{0:T(1024)(128)(2,1)S(1)} %pad_maximum_fusion, ...), channel_id=3, replica_groups=mesh['batch'=4,'seq'=8] {'batch'}, use_global_device_ids=true, to_apply=%region_11.12.clone | all-reduce | flops 9216 | bytes 36864
  627.5 12.3 %all-reduce.10 = (bf16[192]{0:T(256)(128)(2,1)S(1)}, bf16[192]{0:T(256)(128)(2,1)S(1)}, bf16[192]{0:T(256)(128)(2,1)S(1)}, bf16[192]{0:T(256)(128)(2,1)S(1)}, bf...) all-reduce(bf16[192]{0:T(256)(128)(2,1)S(1)} %dynamic-slice.1, ...), channel_id=1, replica_groups=mesh['batch'=4,'seq'=8] {'seq'}, use_global_device_ids=true, to_apply=%region_12.13 | all-reduce | flops 2304 | bytes 9216 | tf_op jit(solution)/shard_map/psum | solution.py:1182
  645.0 32.1 %all-reduce.15.cloned.1.call-done = (bf16[192,2304]{1,0:T(8,128)(2,1)}, bf16[192,768]{1,0:T(8,128)(2,1)}, bf16[192,3072]{1,0:T(8,128)(2,1)}, bf16[768,768]{1,0:T(8,128)(2,1)}) async-done(((bf16[192,2304]{1,0:T(8,128)(2,1)}, bf16[192,768]{1,0:T(8,128)(2,1)}, bf16[192,3072]{1,0:T(8,128)(2,1)}, bf16[768,768]{1,0:T(8,128)(2,1)}), (bf16[192,2304]{1,0:T(8,128)(2,1)}, bf16[192,768]{1,0:T(8,128)(2,1)}, ...) | async-done | bytes 3538960 | tf_op jit(solution)/shard_map/psum | solution.py:1182
  677.0 3.0 convert_element_type.163
  680.1 2.8 convert_element_type.166
  685.1 3.2 copy.44
  (161 shorter events, 40.1 us)
Async XLA Ops:
  7.2 6.8 copy-start.23
  7.2 6.8 copy-start.24
  7.2 6.8 copy-start.25
  7.2 6.8 copy-start.26
  7.2 6.8 copy-start.27
  7.3 6.8 copy-start.21
  7.3 217.5 %all-to-all-start.1 = ((bf16[12,128,768]{2,1,0:T(8,128)(2,1)}), bf16[12,128,768]{2,1,0:T(8,128)(2,1)}, u32[]{:S(2)}, u32[]{:S(2)}) async-start(bf16[12,128,768]{2,1,0:T(8,128)(2,1)} %param.33), calls=%async_computation.1 | async-start | bytes 4718592 | tf_op jit(solution)/shard_map/all_to_all | solution.py:1096
  12.6 420.4 %reduce-scatter.7.cloned.1.call-start = ((), (), s32[]{:S(2)}) async-start(), calls=%async_computation.8 | async-start | bytes 1474560 | tf_op jit(solution)/shard_map/reduce_scatter | solution.py:1181
  154.4 52.4 %copy-start.13 = (f32[1536]{0:T(1024)}, f32[1536]{0:T(1024)S(1)}, u32[]{:S(2)}) copy-start(f32[1536]{0:T(1024)S(1)} %add_rsqrt_fusion.1) | copy-start | bytes 18436
  154.5 52.3 %copy-start.15 = (f32[768]{0:T(1024)}, f32[768]{0:T(1024)S(1)}, u32[]{:S(2)}) copy-start(f32[768]{0:T(1024)S(1)} %mul.151) | copy-start | bytes 9220
  154.6 52.3 %copy-start.17 = (f32[768]{0:T(1024)}, f32[768]{0:T(1024)S(1)}, u32[]{:S(2)}) copy-start(f32[768]{0:T(1024)S(1)} %add.166) | copy-start | bytes 9220
  157.5 49.3 %copy-start.5 = (bf16[1536,768]{1,0:T(8,128)(2,1)}, bf16[1536,768]{1,0:T(8,128)(2,1)S(1)}, u32[]{:S(2)}) copy-start(bf16[1536,768]{1,0:T(8,128)(2,1)S(1)} %fusion.24) | copy-start | bytes 7077892
  157.6 49.3 %copy-start.20 = (f32[4,192]{1,0:T(4,128)S(1)}, f32[4,192]{1,0:T(4,128)}, u32[]{:S(2)}) copy-start(f32[4,192]{1,0:T(4,128)} %get-tuple-element.57) | copy-start | bytes 9220
  157.6 49.3 %copy-start.10 = (f32[1536]{0:T(1024)S(1)}, f32[1536]{0:T(1024)}, u32[]{:S(2)}) copy-start(f32[1536]{0:T(1024)} %copy-done.9) | copy-start | bytes 18436
  207.0 14.7 %copy-start.19 = (f32[4,192]{1,0:T(4,128)S(1)}, f32[4,192]{1,0:T(4,128)}, u32[]{:S(2)}) copy-start(f32[4,192]{1,0:T(4,128)} %get-tuple-element.55) | copy-start | bytes 9220
  207.0 14.8 %copy-start.18 = (f32[4,192]{1,0:T(4,128)S(1)}, f32[4,192]{1,0:T(4,128)}, u32[]{:S(2)}) copy-start(f32[4,192]{1,0:T(4,128)} %get-tuple-element.56) | copy-start | bytes 9220
  230.2 9.5 %slice-start.4 = ((s8[4718592]{0:T(1024)(128)(4,1)}), s8[4194304]{0:T(1024)(128)(4,1)S(1)}, s32[]{:S(2)}) async-start(s8[4718592]{0:T(1024)(128)(4,1)} %bitcast.72), calls=%async_computation.16 | async-start | bytes 8388608
  232.6 7.1 %slice-start.5 = ((s8[4718592]{0:T(1024)(128)(4,1)}), s8[524288]{0:T(1024)(128)(4,1)S(1)}, s32[]{:S(2)}) async-start(s8[4718592]{0:T(1024)(128)(4,1)} %bitcast.72), calls=%async_computation.17 | async-start | bytes 1048576
  232.6 22.7 %slice-start = ((s8[4718592]{0:T(1024)(128)(4,1)}), s8[4194304]{0:T(1024)(128)(4,1)S(1)}, s32[]{:S(2)}) async-start(s8[4718592]{0:T(1024)(128)(4,1)} %bitcast.59), calls=%async_computation.12 | async-start | bytes 8388608
  239.8 15.6 %slice-start.1 = ((s8[4718592]{0:T(1024)(128)(4,1)}), s8[524288]{0:T(1024)(128)(4,1)S(1)}, s32[]{:S(2)}) async-start(s8[4718592]{0:T(1024)(128)(4,1)} %bitcast.59), calls=%async_computation.13 | async-start | bytes 1048576
  239.8 15.6 %copy-start.14 = (f32[1536]{0:T(1024)S(1)}, f32[1536]{0:T(1024)}, u32[]{:S(2)}) copy-start(f32[1536]{0:T(1024)} %copy-done.13) | copy-start | bytes 18436
  239.8 15.6 %copy-start.16 = (f32[768]{0:T(1024)S(1)}, f32[768]{0:T(1024)}, u32[]{:S(2)}) copy-start(f32[768]{0:T(1024)} %copy-done.15) | copy-start | bytes 9220
  255.3 17.6 %copy-start.1 = (bf16[1536,3072]{1,0:T(8,128)(2,1)}, bf16[1536,3072]{1,0:T(8,128)(2,1)S(1)}, u32[]{:S(2)}) copy-start(bf16[1536,3072]{1,0:T(8,128)(2,1)S(1)} %fusion.8) | copy-start | bytes 28311556
  282.8 150.3 %reduce-scatter.5.cloned.1.call-start = ((), (), s32[]{:S(2)}) async-start(), calls=%async_computation.7 | async-start | bytes 4423680 | tf_op jit(solution)/shard_map/reduce_scatter | solution.py:1181
  356.8 153.5 %reduce-scatter.11.cloned.1.call-start = ((), (), s32[]{:S(2)}) async-start(), calls=%async_computation.10 | async-start | bytes 5898240 | tf_op jit(solution)/shard_map/reduce_scatter | solution.py:1181
  370.1 228.2 %reduce-scatter.9.cloned.1.call-start = ((), (), s32[]{:S(2)}) async-start(), calls=%async_computation.9 | async-start | bytes 5898240 | tf_op jit(solution)/shard_map/reduce_scatter | solution.py:1181
  384.7 7.4 %slice-start.2 = ((s8[4718592]{0:T(1024)(128)(4,1)}), s8[524288]{0:T(1024)(128)(4,1)S(1)}, s32[]{:S(2)}) async-start(s8[4718592]{0:T(1024)(128)(4,1)} %bitcast.62), calls=%async_computation.14 | async-start | bytes 1048576
  428.0 170.3 %copy-start.36 = (u32[32]{0:T(128)S(1)}, u32[32]{0:T(128)}, u32[]{:S(2)}) copy-start(u32[32]{0:T(128)} %constant.121) | copy-start | bytes 388
  428.0 216.9 %all-to-all-start = ((bf16[12,128,768]{2,1,0:T(8,128)(2,1)}), bf16[12,128,768]{2,1,0:T(8,128)(2,1)}, u32[]{:S(2)}, u32[]{:S(2)}) async-start(bf16[12,128,768]{2,1,0:T(8,128)(2,1)} %bitcast.61), calls=%async_computation | async-start | bytes 4718592 | tf_op jit(solution)/shard_map/all_to_all | solution.py:1096
  432.8 244.3 %all-reduce.15.cloned.1.call-start = ((), (), s32[]{:S(2)}) async-start(), calls=%async_computation.11 | async-start | bytes 7077888 | tf_op jit(solution)/shard_map/psum | solution.py:1182
  600.2 8.4 %copy-start.22 = (bf16[768]{0:T(1024)(128)(2,1)S(1)}, bf16[768]{0:T(1024)(128)(2,1)}, u32[]{:S(2)}) copy-start(bf16[768]{0:T(1024)(128)(2,1)} %get-tuple-element.50) | copy-start | bytes 4612
  677.0 7.2 %copy-start.8 = (bf16[192,768]{1,0:T(8,128)(2,1)S(1)}, bf16[192,768]{1,0:T(8,128)(2,1)}, u32[]{:S(2)}) copy-start(bf16[192,768]{1,0:T(8,128)(2,1)} %get-tuple-element.71) | copy-start | bytes 884740
  (18 other events, 77.1 us)
Sparse Core Ops, SparseCore 0:
  282.9 35.3 reduce-scatter.6
  356.9 65.5 reduce-scatter.4
  424.8 85.5 reduce-scatter.10
  512.5 85.7 reduce-scatter.8
  601.8 75.1 all-reduce.14

commit v2 on v1

--- a/solution.py
+++ b/solution.py
@@ -869,7 +869,119 @@
     )(tokens, pos, attend_weight, vectors, output_weight, expand_weight, reduce_weight)
 
 
-def attend_back_kernel(
+def add_into(target, at, parts):
+    total = target[at].astype(f32)
+    for part in parts:
+        total = total + part.astype(f32)
+    target[at] = total.astype(target.dtype)
+
+
+class Reducer:
+    def __init__(self, me, src_half, own, near, mid, last, done, sems, tower_first):
+        self.me, self.src_half = me, src_half
+        self.own, self.near, self.mid, self.last, self.done = own, near, mid, last, done
+        (self.near_s, self.near_r, self.mid_s, self.mid_r, self.last_s, self.last_r) = sems[:6]
+        (self.back_s, self.back_r, self.side_s, self.side_r) = sems[6:10]
+        self.loc = sems[10]
+        self.tower_first = tower_first
+        self.depth, self.chips = own.shape[0], own.shape[1]
+
+    def near_copy(self):
+        me = self.me
+        return far_copy(
+            self.src_half(1 - me.core), self.near, (self.near_s, self.near_r), 0, me.sibling()
+        )
+
+    def own_copy(self):
+        return pltpu.make_async_copy(self.src_half(self.me.core), self.own, self.loc.at[0])
+
+    def begin(self):
+        self.near_copy().start()
+        self.own_copy().start()
+
+    def fold_near(self):
+        self.own_copy().wait()
+        self.near_copy().wait()
+
+        @pl.loop(0, self.depth)
+        def _(a):
+            for b in range(self.chips):
+                add_into(self.own, (a, b), [self.near[a, b]])
+
+    def mid_copy(self, k):
+        me = self.me
+        if self.tower_first:
+            src, device = self.own.at[me.z_at(k)], me.tower(k)
+        else:
+            src, device = self.own.at[:, me.chip_at(k)], me.plane(k)
+        return far_copy(src, self.mid.at[k - 1], (self.mid_s, self.mid_r), k - 1, device)
+
+    def mid_range(self):
+        return range(1, self.depth if self.tower_first else self.chips)
+
+    def send_mid(self):
+        for k in self.mid_range():
+            self.mid_copy(k).start()
+
+    def fold_mid(self):
+        me = self.me
+        for k in self.mid_range():
+            self.mid_copy(k).wait()
+        if self.tower_first:
+            for b in range(self.chips):
+                add_into(self.own, (me.z, b), [self.mid[k - 1, b] for k in self.mid_range()])
+        else:
+            for a in range(self.depth):
+                add_into(self.own, (a, me.chip), [self.mid[k - 1, a] for k in self.mid_range()])
+
+    def last_range(self):
+        return range(1, self.chips if self.tower_first else self.depth)
+
+    def last_copy(self, k):
+        me = self.me
+        if self.tower_first:
+            src, device = self.own.at[me.z, me.chip_at(k)], me.plane(k)
+        else:
+            src, device = self.own.at[me.z_at(k), me.chip], me.tower(k)
+        return far_copy(src, self.last.at[k - 1], (self.last_s, self.last_r), k - 1, device)
+
+    def send_last(self):
+        for k in self.last_range():
+            self.last_copy(k).start()
+
+    def fold_last(self):
+        me = self.me
+        for k in self.last_range():
+            self.last_copy(k).wait()
+        total = self.own[me.z, me.chip].astype(f32)
+        for k in self.last_range():
+            total = total + self.last[k - 1].astype(f32)
+        self.done[me.core, me.chip] = total.astype(bf16)
+
+    def back_copy(self, k):
+        me = self.me
+        spot = self.done.at[me.core, me.chip]
+        return far_copy(spot, spot, (self.back_s, self.back_r), k - 1, me.plane(k))
+
+    def send_back(self):
+        for k in range(1, self.chips):
+            self.back_copy(k).start()
+
+    def side_copy(self):
+        me = self.me
+        spot = self.done.at[me.core]
+        return far_copy(spot, spot, (self.side_s, self.side_r), 0, me.sibling())
+
+    def send_side(self):
+        for k in range(1, self.chips):
+            self.back_copy(k).wait()
+        self.side_copy().start()
+
+    def finish(self):
+        self.side_copy().wait()
+
+
+def back_kernel(
     chips,
     depth,
     heads,
@@ -880,9 +992,19 @@
     p_ref,
     pos_ref,
     x_ref,
-    g_out,
-    dw_out,
-    db_out,
+    aw_ref,
+    res_ref,
+    go_ref,
+    ge_ref,
+    gr_ref,
+    gv_ref,
+    token_out,
+    aw_out,
+    ow_out,
+    ew_out,
+    rw_out,
+    vec_out,
+    bias_out,
     dbuf,
     qs,
     ks,
@@ -890,19 +1012,57 @@
     ps,
     posbuf,
     xbuf,
+    wbuf,
+    rbuf,
     ds,
     gs,
     gbuf,
+    gfar,
+    tbuf,
     dw,
-    db,
+    dwb,
+    amid,
+    alast,
+    adone,
+    o_own,
+    o_near,
+    o_mid,
+    o_last,
+    o_done,
+    e_own,
+    e_near,
+    e_mid,
+    e_last,
+    e_done,
+    r_own,
+    r_near,
+    r_mid,
+    r_last,
+    r_done,
+    a32,
+    o32,
+    e32,
+    r32,
+    vbuf,
+    vgot,
+    bbuf,
+    bgot,
     d_s,
     d_r,
     g_s,
     g_r,
-    loc,
+    t_s,
+    t_r,
+    load,
+    out_sem,
+    v_s,
+    v_r,
+    b_s,
+    b_r,
+    *sems,
 ):
     me = Place(chips, depth)
-    core = me.core
+    core, chip = me.core, me.chip
     per = d_ref.shape[1]
     cluster, width = d_ref.shape[2], d_ref.shape[3]
     half = width // 2
@@ -911,135 +1071,408 @@
     blocks = 2 * chips
     share = cluster // blocks
     me.greet()
+    groups = [sems[n * 11 : (n + 1) * 11] for n in range(4)]
+    wide = ge_ref.shape[2] // (2 * chips)
+
+    def out_half(c):
+        return go_ref.at[:, pl.ds(c * chips, chips)]
+
+    def reduce_half(c):
+        return gr_ref.at[:, pl.ds(c * chips, chips)]
+
+    def expand_half(c):
+        return ge_ref.at[:, :, pl.ds(multiple(c * chips * wide, 128), chips * wide)]
+
+    red = Reducer(me, reduce_half, r_own, r_near, r_mid, r_last, r_done, groups[0], True)
+    exp = Expander(me, expand_half, e_own, e_near, e_mid, e_last, e_done, groups[1], False)
+    out = Reducer(me, out_half, o_own, o_near, o_mid, o_last, o_done, groups[2], False)
+    att = Reducer(me, None, dwb, None, amid, alast, adone, groups[3], False)
+
     theirs = pl.ds(multiple((1 - core) * half, 128), half)
     far = far_copy(d_ref.at[:, :, :, theirs], dbuf.at[core], (d_s, d_r), 0, me.sibling())
     far.start()
-    local = []
-
-    def keep(src, dst):
-        copy = pltpu.make_async_copy(src, dst, loc.at[len(local)])
+    first = [
+        pltpu.make_async_copy(
+            d_ref.at[:, :, :, pl.ds(multiple(core * half, 128), half)], dbuf.at[core], load.at[12]
+        ),
+        pltpu.make_async_copy(pos_ref, posbuf, load.at[13]),
+        pltpu.make_async_copy(aw_ref, wbuf, load.at[14]),
+        pltpu.make_async_copy(gv_ref, vbuf, load.at[15]),
+    ]
+
+    def loads(i, slot):
+        span = pl.ds(i * pairs, pairs)
+        pieces = (
+            (q_ref.at[span], qs),
+            (k_ref.at[span], ks),
+            (v_ref.at[span], vs),
+            (p_ref.at[span], ps),
+        )
+        return [
+            pltpu.make_async_copy(src, dst.at[slot], load.at[slot * 4 + n])
+            for n, (src, dst) in enumerate(pieces)
+        ]
+
+    def load_x(i):
+        return pltpu.make_async_copy(x_ref.at[:, :, i], xbuf, load.at[8])
+
+    def load_r(i):
+        return pltpu.make_async_copy(res_ref.at[:, i], rbuf, load.at[9])
+
+    for copy in first + loads(0, 0) + [load_x(0)]:
         copy.start()
-        local.append(copy)
-
-    keep(d_ref.at[:, :, :, pl.ds(multiple(core * half, 128), half)], dbuf.at[core])
-    keep(pos_ref, posbuf)
-    keep(q_ref, qs)
-    keep(k_ref, ks)
-    keep(v_ref, vs)
-    keep(p_ref, ps)
-    keep(x_ref, xbuf)
-    for copy in local[:6]:
-        copy.wait()
-    far.wait()
+    red.begin()
+    exp.begin()
+    out.begin()
+
     slots = lax.broadcasted_iota(jnp.int32, (cluster, cluster), 0)
     low = lax.broadcasted_iota(jnp.int32, (cluster, 128), 1) < size
     scale = size ** (-0.5)
-    db[...] = jnp.zeros_like(db)
-    dw[...] = jnp.zeros_like(dw)
+    bbuf[...] = jnp.zeros_like(bbuf)
+    for copy in first:
+        copy.wait()
+    far.wait()
 
     def tables(jj, i, pair, part):
-        first = part * heads + core * (heads // 2) + 2 * pair
+        begin = part * heads + core * (heads // 2) + 2 * pair
         return [
-            one_hot(posbuf[jj // chips, jj % chips, i, pl.ds(first + h, 1), :], slots)
+            one_hot(posbuf[jj // chips, jj % chips, i, pl.ds(begin + h, 1), :], slots)
             for h in range(2)
         ]
 
-    for copy in local[6:]:
-        copy.wait()
-
-    @pl.loop(0, per)
-    def _(i):
+    def clusters(i, slot, pair):
+        lanes = pl.ds(multiple(pair * 128, 128), 128)
+        for jj in range(blocks):
+            tq = jnp.concatenate(tables(jj, i, pair, 0), axis=1)
+            rows = stack_lanes(dbuf[jj // chips, jj % chips, i, :, lanes], low)
+            ds[:, jj * share : (jj + 1) * share, :] = (
+                dot_rows(tq, rows).astype(bf16).reshape(blocks, share, 128)
+            )
+        for c in range(blocks):
+            d = ds[c]
+            probs = ps[slot, pair, c]
+            slope = dot_lanes(d, stack_lanes(vs[slot, pair, c], low))
+            broad = probs.astype(f32)
+            halves = []
+            for h in range(2):
+                span = slice(h * cluster, (h + 1) * cluster)
+                inner = jnp.sum(broad[:, span] * slope[:, span], axis=1, keepdims=True)
+                halves.append((broad[:, span] * (slope[:, span] - inner)).astype(bf16))
+            grads = jnp.concatenate(halves, axis=1)
+            gq = dot_rows(grads, stack_lanes(ks[slot, pair, c], low)) * scale
+            gk = dot_first(grads, qs[slot, pair, c]) * scale
+            gv = dot_first(probs, d)
+            gs[0, c] = gq.astype(bf16)
+            gs[1, c] = jnp.where(low, gk[:cluster], gk[cluster:]).astype(bf16)
+            gs[2, c] = jnp.where(low, gv[:cluster], gv[cluster:]).astype(bf16)
+        for jj in range(blocks):
+            for part in range(3):
+                if part < 2:
+                    table = jnp.concatenate(tables(jj, i, pair, part), axis=0)
+                rows = gs[part, :, jj * share : (jj + 1) * share, :].reshape(cluster, 128)
+                back = dot_first(table, stack_lanes(rows, low))
+                to = pl.ds(multiple(part * half + pair * 128, 128), 128)
+                gbuf[slot, jj // chips, jj % chips, :, to] = back.astype(bf16)
+
+    def give(slot):
+        return far_copy(gbuf.at[slot, 1 - core], gfar.at[slot], (g_s, g_r), slot, me.sibling())
+
+    def token_copy(i, slot, k):
+        return far_copy(
+            tbuf.at[slot, me.chip_at(k)],
+            token_out.at[chip * per + i],
+            (t_s, t_r),
+            i * (chips - 1) + k - 1,
+            me.plane(k),
+        )
+
+    def token_keep(i, slot):
+        return pltpu.make_async_copy(
+            tbuf.at[slot, chip], token_out.at[chip * per + i], out_sem.at[i]
+        )
+
+    def token_rows(i, slot):
+        load_r(i).wait()
+        give(slot).wait()
+        for j in range(chips):
+            near = dot_lanes(gbuf[slot, core, j], wbuf[core])
+            distant = dot_lanes(gfar[slot, j], wbuf[1 - core])
+            tbuf[slot, j] = (rbuf[j] + near + distant).astype(bf16)
+        token_keep(i, slot).start()
+        for k in range(1, chips):
+            token_copy(i, slot, k).start()
+
+    for i in range(per):
+        slot = i % 2
+        for copy in loads(i, slot):
+            copy.wait()
+        if i >= 1:
+            token_rows(i - 1, 1 - slot)
+        load_r(i).start()
+        if i + 1 < per:
+            for copy in loads(i + 1, 1 - slot):
+                copy.start()
+
         @pl.loop(0, pairs)
         def _(pair):
-            at = i * pairs + pair
-            lanes = pl.ds(multiple(pair * 128, 128), 128)
-            for jj in range(blocks):
-                tq = jnp.concatenate(tables(jj, i, pair, 0), axis=1)
-                rows = stack_lanes(dbuf[jj // chips, jj % chips, i, :, lanes], low)
-                ds[:, jj * share : (jj + 1) * share, :] = (
-                    dot_rows(tq, rows).astype(bf16).reshape(blocks, share, 128)
-                )
-            for c in range(blocks):
-                d = ds[c]
-                probs = ps[at, c]
-                slope = dot_lanes(d, stack_lanes(vs[at, c], low))
-                wide = probs.astype(f32)
-                halves = []
-                for h in range(2):
-                    span = slice(h * cluster, (h + 1) * cluster)
-                    inner = jnp.sum(wide[:, span] * slope[:, span], axis=1, keepdims=True)
-                    halves.append((wide[:, span] * (slope[:, span] - inner)).astype(bf16))
-                grads = jnp.concatenate(halves, axis=1)
-                gq = dot_rows(grads, stack_lanes(ks[at, c], low)) * scale
-                gk = dot_first(grads, qs[at, c]) * scale
-                gv = dot_first(probs, d)
-                gs[0, c] = gq.astype(bf16)
-                gs[1, c] = jnp.where(low, gk[:cluster], gk[cluster:]).astype(bf16)
-                gs[2, c] = jnp.where(low, gv[:cluster], gv[cluster:]).astype(bf16)
-            for jj in range(blocks):
-                for part in range(3):
-                    if part < 2:
-                        table = jnp.concatenate(tables(jj, i, pair, part), axis=0)
-                    rows = gs[part, :, jj * share : (jj + 1) * share, :].reshape(cluster, 128)
-                    back = dot_first(table, stack_lanes(rows, low))
-                    to = pl.ds(multiple(part * half + pair * 128, 128), 128)
-                    gbuf[jj // chips, jj % chips, i, :, to] = back.astype(bf16)
-
+            clusters(i, slot, pair)
+
+            if i == 0:
+
+                @pl.when(pair == 0)
+                def _():
+                    red.fold_near()
+                    red.send_mid()
+                    exp.fold_near()
+                    exp.send_mid()
+                    out.fold_near()
+                    out.send_mid()
+
+        if i >= 2:
+            token_keep(i - 2, slot).wait()
+            for k in range(1, chips):
+                token_copy(i - 2, slot, k).wait()
+        give(slot).start()
+        load_x(i).wait()
         for b in range(2):
-            x = jnp.concatenate([xbuf[b, j, i] for j in range(chips)], axis=0)
-            g = jnp.concatenate([gbuf[b, j, i] for j in range(chips)], axis=0)
-            dw[...] += dot_first(x, g)
-            db[0:1, :] += jnp.sum(g.astype(f32), axis=0, keepdims=True)
-
-    give = far_copy(gbuf.at[1 - core], g_out.at[core], (g_s, g_r), 0, me.sibling())
-    give.start()
-    tail = []
-    for n, (src, dst) in enumerate(
-        ((gbuf.at[core], g_out.at[core]), (dw, dw_out), (db, db_out))
-    ):
-        tail.append(pltpu.make_async_copy(src, dst, loc.at[n]))
-        tail[-1].start()
-    for copy in tail:
+            x = jnp.concatenate([xbuf[b, j] for j in range(chips)], axis=0)
+            g = jnp.concatenate([gbuf[slot, b, j] for j in range(chips)], axis=0)
+            term = dot_first(x, g)
+            if i == 0 and b == 0:
+                dw[...] = term
+            else:
+                dw[...] += term
+            bbuf[0:1, :] += jnp.sum(g.astype(f32), axis=0, keepdims=True)
+        if i + 1 < per:
+            load_x(i + 1).start()
+        if i == per - 2:
+            exp.fold_mid()
+            exp.send_last()
+            out.fold_mid()
+            out.send_last()
+
+    rows = dwb.shape[2]
+    for a in range(depth):
+        for b in range(chips):
+            begin = (a * chips + b) * rows
+            dwb[a, b] = dw[begin : begin + rows, :].astype(bf16)
+    att.send_mid()
+    token_rows(per - 1, (per - 1) % 2)
+    exp.fold_last()
+    exp.send_back()
+    out.fold_last()
+    out.send_back()
+    red.fold_mid()
+    red.send_last()
+    for hop in range(3):
+        for vec, got, s, r, skip in ((vbuf, vgot, v_s, v_r, -1), (bbuf, bgot, b_s, b_r, 0)):
+            if hop == skip:
+                continue
+            if hop == 0:
+                copies = [far_copy(vec, got.at[0], (s, r), 0, me.sibling())]
+                begin = 0
+            elif hop == 1:
+                begin = 1
+                copies = [
+                    far_copy(vec, got.at[k], (s, r), k, me.plane(k)) for k in range(1, chips)
+                ]
+            else:
+                begin = chips
+                copies = [
+                    far_copy(vec, got.at[chips + k - 1], (s, r), chips + k - 1, me.tower(k))
+                    for k in range(1, depth)
+                ]
+            for copy in copies:
+                copy.start()
+            for copy in copies:
+                copy.wait()
+            total = vec[...]
+            for n in range(len(copies)):
+                total = total + got[begin + n]
+            vec[...] = total
+    att.fold_mid()
+    att.send_last()
+    last = [pltpu.make_async_copy(vbuf, vec_out, out_sem.at[per])]
+    last[-1].start()
+    share_bias = far_copy(bbuf, bias_out.at[core], (b_s, b_r), 0, me.sibling())
+    share_bias.start()
+    last.append(pltpu.make_async_copy(bbuf, bias_out.at[core], out_sem.at[per + 1]))
+    last[-1].start()
+    red.fold_last()
+    red.send_back()
+    exp.send_side()
+    out.send_side()
+    att.fold_last()
+    att.send_back()
+    red.send_side()
+    exp.finish()
+    tall = e_done.shape[2]
+    for c in range(2):
+        for p in range(chips):
+            at = (c * chips + p) * wide
+            e32[:, at : at + wide] = e_done[c, p].astype(f32)
+    last.append(pltpu.make_async_copy(e32, ew_out, out_sem.at[per + 2]))
+    last[-1].start()
+    out.finish()
+    o32[...] = o_done[...].astype(f32)
+    last.append(pltpu.make_async_copy(o32, ow_out, out_sem.at[per + 3]))
+    last[-1].start()
+    red.finish()
+    r32[...] = r_done[...].astype(f32)
+    last.append(pltpu.make_async_copy(r32, rw_out, out_sem.at[per + 4]))
+    last[-1].start()
+    att.send_side()
+    att.finish()
+    for c in range(2):
+        for p in range(chips):
+            for part in range(3):
+                to = (2 * part + c) * half
+                a32[p * rows : (p + 1) * rows, to : to + half] = adone[
+                    c, p, :, part * half : (part + 1) * half
+                ].astype(f32)
+    last.append(pltpu.make_async_copy(a32, aw_out, out_sem.at[per + 5]))
+    last[-1].start()
+    for i in range(max(per - 2, 0), per):
+        token_keep(i, i % 2).wait()
+        for k in range(1, chips):
+            token_copy(i, i % 2, k).wait()
+    share_bias.wait()
+    for copy in last:
         copy.wait()
-    give.wait()
-
-
-def attend_back(grad_context, q, k, v, p, pos, x, depth, heads):
+
+
+class Expander(Reducer):
+    def __init__(self, me, src_half, own, near, mid, last, done, sems, tower_first):
+        self.wide = done.shape[3]
+        Reducer.__init__(self, me, src_half, own, near, mid, last, done, sems, tower_first)
+        self.chips = done.shape[1]
+
+    def lanes(self, chip):
+        return pl.ds(multiple(chip * self.wide, 128), self.wide)
+
+    def fold_near(self):
+        self.own_copy().wait()
+        self.near_copy().wait()
+
+        @pl.loop(0, self.depth)
+        def _(a):
+            add_into(self.own, a, [self.near[a]])
+
+    def mid_copy(self, k):
+        me = self.me
+        src = self.own.at[:, :, self.lanes(me.chip_at(k))]
+        return far_copy(src, self.mid.at[k - 1], (self.mid_s, self.mid_r), k - 1, me.plane(k))
+
+    def fold_mid(self):
+        me = self.me
+        for k in self.mid_range():
+            self.mid_copy(k).wait()
+        here = self.lanes(me.chip)
+        for a in range(self.depth):
+            total = self.own[a, :, here].astype(f32)
+            for k in self.mid_range():
+                total = total + self.mid[k - 1, a].astype(f32)
+            self.own[a, :, here] = total.astype(bf16)
+
+    def last_copy(self, k):
+        me = self.me
+        src = self.own.at[me.z_at(k), :, self.lanes(me.chip)]
+        return far_copy(src, self.last.at[k - 1], (self.last_s, self.last_r), k - 1, me.tower(k))
+
+    def fold_last(self):
+        me = self.me
+        for k in self.last_range():
+            self.last_copy(k).wait()
+        total = self.own[me.z, :, self.lanes(me.chip)].astype(f32)
+        for k in self.last_range():
+            total = total + self.last[k - 1].astype(f32)
+        self.done[me.core, me.chip] = total.astype(bf16)
+
+
+def back(
+    grad_context, q, k, v, p, pos, x, attend_all, resid, g_out, g_exp, g_red, g_vec, depth, heads
+):
     chips, per, cluster, width = grad_context.shape
     half, blocks, pairs = width // 2, 2 * chips, heads // 4
     dma = pltpu.SemaphoreType.DMA
     anywhere = pl.BlockSpec(memory_space=pl.ANY)
+    quarter = width // depth
+    hidden = g_exp.shape[-1]
+    eighth, tall, wide = quarter // blocks, hidden // depth // blocks, hidden // blocks
+    rows = quarter // chips
+    c, t = chips - 1, depth - 1
     shapes = [
-        ((2, chips, per, cluster, 3 * half), bf16),
-        ((width, 3 * half), f32),
-        ((8, 3 * half), f32),
+        ((chips * per, cluster, width), bf16),
+        ((quarter, 3 * width), f32),
+        ((2, chips, eighth, width), f32),
+        ((quarter, hidden), f32),
+        ((2, chips, tall, width), f32),
+        (g_vec.shape, f32),
+        ((2, 8, 3 * half), f32),
     ]
+    vm = pltpu.VMEM
+    one = dma((1,))
+    reducer = [one, one, dma((c,)), dma((c,)), dma((t,)), dma((t,)), dma((c,)), dma((c,)), one, one, one]
+    tower = [one, one, dma((t,)), dma((t,)), dma((c,)), dma((c,)), dma((c,)), dma((c,)), one, one, one]
     return pl.pallas_call(
-        functools.partial(attend_back_kernel, chips, depth, heads),
+        functools.partial(back_kernel, chips, depth, heads),
         out_shape=[jax.ShapeDtypeStruct(*s) for s in shapes],
-        in_specs=[anywhere] * 7,
-        out_specs=[anywhere] * 3,
+        in_specs=[anywhere] * 13,
+        out_specs=[anywhere] * len(shapes),
         scratch_shapes=[
-            pltpu.VMEM((2, chips, per, cluster, half), bf16),
-            pltpu.VMEM(q.shape, bf16),
-            pltpu.VMEM(q.shape, bf16),
-            pltpu.VMEM(q.shape, bf16),
-            pltpu.VMEM(p.shape, bf16),
-            pltpu.VMEM(pos.shape, jnp.int32),
-            pltpu.VMEM(x.shape, bf16),
-            pltpu.VMEM((blocks, cluster, 128), bf16),
-            pltpu.VMEM((3, blocks, cluster, 128), bf16),
-            pltpu.VMEM(shapes[0][0], bf16),
-            pltpu.VMEM(shapes[1][0], f32),
-            pltpu.VMEM(shapes[2][0], f32),
-            dma((1,)), dma((1,)), dma((1,)), dma((1,)),
-            dma((7,)),
+            vm((2, chips, per, cluster, half), bf16),
+            vm((2, pairs, blocks, cluster, 128), bf16),
+            vm((2, pairs, blocks, cluster, 128), bf16),
+            vm((2, pairs, blocks, cluster, 128), bf16),
+            vm((2, pairs, blocks, cluster, 2 * cluster), bf16),
+            vm(pos.shape, jnp.int32),
+            vm((2, chips, cluster, width), bf16),
+            vm(attend_all.shape, bf16),
+            vm((chips, cluster, width), f32),
+            vm((blocks, cluster, 128), bf16),
+            vm((3, blocks, cluster, 128), bf16),
+            vm((2, 2, chips, cluster, 3 * half), bf16),
+            vm((2, chips, cluster, 3 * half), bf16),
+            vm((2, chips, cluster, width), bf16),
+            vm((width, 3 * half), f32),
+            vm((depth, chips, rows, 3 * half), bf16),
+            vm((c, depth, rows, 3 * half), bf16),
+            vm((t, rows, 3 * half), bf16),
+            vm((2, chips, rows, 3 * half), bf16),
+            vm((depth, chips, eighth, width), bf16),
+            vm((depth, chips, eighth, width), bf16),
+            vm((c, depth, eighth, width), bf16),
+            vm((t, eighth, width), bf16),
+            vm((2, chips, eighth, width), bf16),
+            vm((depth, quarter, chips * wide), bf16),
+            vm((depth, quarter, chips * wide), bf16),
+            vm((c, depth, quarter, wide), bf16),
+            vm((t, quarter, wide), bf16),
+            vm((2, chips, quarter, wide), bf16),
+            vm((depth, chips, tall, width), bf16),
+            vm((depth, chips, tall, width), bf16),
+            vm((t, chips, tall, width), bf16),
+            vm((c, tall, width), bf16),
+            vm((2, chips, tall, width), bf16),
+            vm(shapes[1][0], f32),
+            vm(shapes[2][0], f32),
+            vm(shapes[3][0], f32),
+            vm(shapes[4][0], f32),
+            vm(g_vec.shape, f32),
+            vm((chips + t,) + g_vec.shape, f32),
+            vm((8, 3 * half), f32),
+            vm((chips + t, 8, 3 * half), f32),
+            one, one, dma((2,)), dma((2,)),
+            dma((per * c,)), dma((per * c,)),
+            dma((16,)), dma((per + 6,)),
+            dma((chips + t,)), dma((chips + t,)), dma((chips + t,)), dma((chips + t,)),
+            *tower, *reducer, *reducer, *reducer,
         ],
         compiler_params=pltpu.CompilerParams(
-            collective_id=2, has_side_effects=True, vmem_limit_bytes=60 * 2**20
+            collective_id=2, has_side_effects=True, vmem_limit_bytes=63 * 2**20
         ),
-        name="attend_back",
-    )(grad_context, q, k, v, p, pos, x)
+        name="back",
+    )(grad_context, q, k, v, p, pos, x, attend_all, resid, g_out, g_exp, g_red, g_vec)
 
 
 def places(rank, cluster, share):
@@ -1156,47 +1589,62 @@
     grad_output_bias = jnp.sum(grad_branch_one, axis=0, dtype=f32)
     grad_output = transpose_left(context, grad_branch_one)
     grad_context = transpose_right(grad_branch_one, output_full).astype(bf16)
-    grads, grad_attend_half, grad_bias_half = attend_back(
-        grad_context.reshape(chips, per, cluster, width), qs, ks, vs, ps, pos_all, x_all, depth, heads
-    )
-    grads = grads.reshape(2, rows, 3 * half)
-    token_grad = grad_resid_one
-    for c in range(2):
-        token_grad = token_grad + transpose_right(grads[c], attend_all[c])
-    token_grad = swap(token_grad.astype(bf16).reshape(seqs, cluster, width))
-
-    def spread(part):
-        zero = jnp.zeros_like(part)
-        pick = core == 0
-        return jnp.where(pick, part, zero), jnp.where(pick, zero, part)
-
-    columns = []
-    for part in range(3):
-        columns += spread(grad_attend_half[:, part * half : (part + 1) * half])
-    grad_attend = jnp.concatenate(columns, axis=1)
-    grad_query_bias = jnp.concatenate(spread(grad_bias_half[0, :half]))
-    grad_value_bias = jnp.concatenate(spread(grad_bias_half[0, 2 * half :]))
-
-    def owned(grad):
-        part = lax.psum_scatter(grad.astype(bf16), "batch", scatter_dimension=0, tiled=True)
-        return lax.psum(part, "seq").astype(f32)
-
+    vector_grads = jnp.concatenate(
+        [
+            grad_output_bias,
+            grad_first_gain,
+            grad_first_shift,
+            grad_reduce_bias,
+            grad_second_gain,
+            grad_second_shift,
+            grad_expand_bias,
+        ]
+    )
+    lanes = -(-vector_grads.shape[0] // 1024) * 8
+    vector_grads = jnp.pad(vector_grads, (0, lanes * 128 - vector_grads.shape[0])).reshape(lanes, 128)
+    layer_out, grad_context = lax.optimization_barrier((layer_out, grad_context))
+    token_grad, aw_grad, ow_grad, ew_grad, rw_grad, vec_sum, bias_sum = back(
+        grad_context.reshape(chips, per, cluster, width),
+        qs,
+        ks,
+        vs,
+        ps,
+        pos_all,
+        x_all,
+        attend_all,
+        grad_resid_one.reshape(chips, per, cluster, width),
+        grad_output.astype(bf16).reshape(depth, owners, -1, width),
+        grad_expand.astype(bf16).reshape(depth, quarter, -1),
+        grad_reduce.astype(bf16).reshape(depth, owners, -1, width),
+        vector_grads,
+        depth,
+        heads,
+    )
+    z = lax.axis_index("batch")
+    vec_sum = vec_sum.reshape(-1)
+    six = lax.dynamic_slice_in_dim(vec_sum[: 6 * width].reshape(6, width), z * quarter, quarter, 1)
+    up = vec_sum[6 * width :]
+    tall = expand_bias.shape[0]
+    up = lax.dynamic_slice_in_dim(up, z * tall, tall, 0)
+    both = jnp.concatenate([bias_sum[0, 0], bias_sum[1, 0]]).reshape(2, 3, half)
+    query_value = jnp.transpose(both, (1, 0, 2)).reshape(3, width)
+    query_value = lax.dynamic_slice_in_dim(query_value, z * quarter, quarter, 1)
     return (
         layer_out,
         token_grad,
-        owned(grad_attend),
-        owned(grad_query_bias),
-        owned(grad_value_bias),
-        owned(grad_output),
-        owned(grad_output_bias),
-        owned(grad_first_gain),
-        owned(grad_first_shift),
-        owned(grad_expand),
-        owned(grad_expand_bias),
-        owned(grad_reduce),
-        owned(grad_reduce_bias),
-        owned(grad_second_gain),
-        owned(grad_second_shift),
+        aw_grad,
+        query_value[0],
+        query_value[2],
+        ow_grad.reshape(quarter, width),
+        six[0],
+        six[1],
+        six[2],
+        ew_grad,
+        up,
+        rw_grad.reshape(-1, width),
+        six[3],
+        six[4],
+        six[5],
     )
 
 

time: 706 us -> 493 us (0.70)
  waiting for transfers between devices: 197 us -> 15.5 us
  Pallas kernels: 188 us -> 275 us
  blocking collectives: 62.8 us -> 0 us
  other arithmetic: 55.1 us -> 25.1 us
  between operations: 16 us -> 1.8 us
  matrix products: 142 us -> 132 us
    reduce_scatter x4 -> x0, waiting for transfers between devices: 165 us -> none  [owned(): lax.psum_scatter(grad.astype(bf16), 'batch', scatter_dimension=0, tiled=T...]
    pallas_call x1, Pallas kernels: 57.9 us -> 145 us  [back(): pl.pallas_call(functools.partial(back_kernel, chips, depth, heads), out_s...]
    all_to_all x1 -> x0, blocking collectives: 32.3 us -> none  [swap(): lax.all_to_all(x, 'seq', split_axis=0, concat_axis=0, tiled=True, axis_in...]
    psum x1 -> x0, waiting for transfers between devices: 32.1 us -> none  [owned(): return lax.psum(part, 'seq').astype(f32)]
    unnamed x1 -> x0, blocking collectives: 18.2 us -> none
    all_to_all x2, waiting for transfers between devices: 0.01 us -> 15.5 us  [swap(): lax.all_to_all(x, 'seq', split_axis=0, concat_axis=0, tiled=True, axis_in...]
    convert_element_type x13 -> x0, other arithmetic: 13.2 us -> none  [owned(): return lax.psum(part, 'seq').astype(f32)]
    psum x1 -> x0, blocking collectives: 12.3 us -> none  [owned(): return lax.psum(part, 'seq').astype(f32)]
  transfers between devices with their start and end apart: 7 -> 2, of which waited for: 3 -> 1; matrix products, arithmetic and copies ran while one was open for 21% -> 19% of each run, Pallas kernels for 27% -> 27%
where the time goes in v2:
time: 493 us; the launch traced here: 484 us
  Pallas kernels  275 us (56%)
  matrix products  132 us (27%)
  other arithmetic  25.1 us (5%)
  local copies, waits for them, and re-layouts  24.4 us (5%)
  waiting for transfers between devices  15.5 us (3%)
  starting transfers between devices  10.2 us (2%)
    pallas_call x1, Pallas kernels, back(): pl.pallas_call(functools.partial(back_kernel, chips, depth, heads), out_s...  145 us
    pallas_call x1, Pallas kernels, attend(): pl.pallas_call(functools.partial(attend_kernel, chips, depth, heads), out...  130 us
    dot_general x1, matrix products, per_chip(): pre = jnp.dot(middle_low, expand_full, preferred_element_type=f32) + bias_up  49.2 us
    dot_general x3, matrix products, transpose_right(): lax.dot_general(first, second, (((1,), (1,)), ((), ())), preferred_elemen...  36 us
    dot_general x3, matrix products, transpose_left(): lax.dot_general(first, second, (((0,), (0,)), ((), ())), preferred_elemen...  29.4 us
    all_to_all x2, waiting for transfers between devices, swap(): lax.all_to_all(x, 'seq', split_axis=0, concat_axis=0, tiled=True, axis_in...  15.5 us
    dot_general x1, matrix products, per_chip(): jnp.dot(hidden, reduce_full, preferred_element_type=f32)  14.9 us
    unnamed x96, local copies, waits for them, and re-layouts  14.3 us
  transfers between devices with their start and end apart: 2, of which 1 were waited for; matrix products, arithmetic and copies ran while one was open for 19% of the time, Pallas kernels for 27%

profile of v2, /device:TPU:0, one launch (start us, length us, event | category | flops | bytes accessed | tf_op | source)
XLA Modules:
  0.0 484.4 jit_solution(9265948753717864560)
XLA Ops:
  0.8 5.3 %all-to-all-start.1 = ((bf16[12,128,768]{2,1,0:T(8,128)(2,1)}), bf16[12,128,768]{2,1,0:T(8,128)(2,1)}, u32[]{:S(2)}, u32[]{:S(2)}) async-start(bf16[12,128,768]{2,1,0:T(8,128)(2,1)} %param.33), calls=%async_computation.1 | async-start | bytes 4718592 | tf_op jit(solution)/shard_map/all_to_all | solution.py:1529
  8.4 129.6 %attend.1 = (bf16[2,4,3,128,768]{4,3,2,1,0:T(8,128)(2,1)}, bf16[4,3,128,768]{3,2,1,0:T(8,128)(2,1)}, bf16[9,8,128,128]{3,2,1,0:T(8,128)(2,1)}, bf16[9,8,128,128]...) custom-call(bf16[12,128,768]{2,1,0:T(8,128)(2,1)} %tok_ref.1, ...), custom_call_target="tpu_custom_call" | custom-call | tf_op jit(solution)/shard_map/attend/pallas_call | solution.py:837
  138.0 0.9 slice_bitcast_fusion
  140.4 2.0 constant_dynamic-slice_fusion.2
  142.7 2.3 fusion.40
  145.1 2.1 copy-done
  148.0 2.9 fusion.24
  151.0 49.2 %fusion.2 = (bf16[1536,3072]{1,0:T(8,128)(2,1)}, f32[1536,3072]{1,0:T(8,128)}) fusion(f32[3072]{0:T(1024)S(1)} %add.120, bf16[1536,768]{1,0:T(8,128)(2,1)S(1)} %fusion.24, bf16[768,3072]{1,0:T(8,128)(2,1)} %bitcast.89), kind=kOutput, calls=%fused_computation.4 | convolution fusion | flops 7559184384 | bytes 35401728 | tf_op jit(solution)/shard_map/dot_general | solution.py:1566
  200.4 14.9 %fusion.41 = (f32[1536]{0:T(1024)S(1)}, f32[1536,768]{1,0:T(8,128)}) fusion(f32[768]{0:T(1024)S(1)} %add.124, bf16[1536,3072]{1,0:T(8,128)(2,1)} %get-tuple-element.88, bf16[3072,768]{1,0:T(8,128)(2,1)} %bitcast.91, f32[768]{0:T(1024)} %copy-done.19, f32[768]{0:T(1024)} %copy-done.17, f32[1536]{0:T(1024)} %copy-done.15, f32[1536,768]{1,0:T(8,128)} %copy-done, ...), kind=kOutput, calls=%fused_computation.114 | convolution fusion | flops 7256013312 | bytes 23620608 | tf_op jit(solution)/shard_map/dot_general | solution.py:1569
  215.5 3.0 multiply_reduce_fusion.2
  218.5 4.1 fusion.23
  222.6 2.9 convert_reduce_fusion.1
  225.6 6.5 %convert_reduce_fusion.2 = (f32[768]{0:T(1024)S(1)}, f32[1536,768]{1,0:T(8,128)S(1)}, bf16[1536,768]{1,0:T(8,128)(2,1)}) fusion(f32[1536]{0:T(1024)S(1)} %broadcast_multiply_fusion.2, f32[1536,768]{1,0:T(8,128)} %get-tuple-element.91, f32[1536]{0:T(1024)S(1)} %broadcast_multiply_fusion.3, f32[1536]{0:T(1024)S(1)} %multiply_bitcast_fusion, f32[768]{0:T(1024)S(1)} %mul.167, ...), kind=kLoop, calls=%fused_computation.42 | loop fusion | flops 16514304 | bytes 14189568 | tf_op jit(solution)/shard_map/reduce_sum | solution.py:1577
  232.1 2.1 copy-done.3
  234.3 15.5 %fusion.8 = bf16[1536,3072]{1,0:T(8,128)(2,1)S(1)} fusion(f32[1536,3072]{1,0:T(8,128)} %get-tuple-element.89, bf16[3072,768]{1,0:T(8,128)(2,1)S(1)} %bitcast.94, f32[3072]{0:T(1024)S(1)} %add.120, f32[1536,768]{1,0:T(8,128)S(1)} %get-tuple-element.74), kind=kOutput, calls=%fused_computation.10 | convolution fusion | flops 7300841472 | bytes 37761024 | tf_op jit(solution)/shard_map/dot_general | solution.py:43
  249.9 17.0 %multiply_reduce_fusion = (f32[768]{0:T(1024)S(1)}, f32[1536]{0:T(1024)S(1)}, f32[1536]{0:T(1024)S(1)}, f32[768]{0:T(1024)S(1)}, f32[1536,768]{1,0:T(8,128)}) fusion(f32[1536,768]{1,0:T(8,128)S(1)} %bitcast.69, f32[1536]{0:T(1024)S(1)} %copy-done.16, f32[1536]{0:T(1024)S(1)} %copy-done.12, f32[768]{0:T(1024)S(1)} %copy-done.18, f32[1536,768]{1,0:T(8,128)} %copy-done.3, ...), kind=kOutput, calls=%fused_computation.43 | convolution fusion | flops 7259548672 | bytes 28345344 | tf_op jit(solution)/shard_map/dot_general | solution.py:43
  266.9 1.8 convert_reduce_fusion
  268.7 13.3 %convolution_convert_fusion = bf16[3072,768]{1,0:T(8,128)(2,1)} fusion(bf16[1536,3072]{1,0:T(8,128)(2,1)} %get-tuple-element.88, f32[1536,768]{1,0:T(8,128)} %copy-done.3), kind=kOutput, calls=%fused_computation.27 | convolution fusion | flops 7251296256 | bytes 18874368 | tf_op jit(solution)/shard_map/dot_general | solution.py:37
  282.1 1.7 convert_reduce_fusion.3
  283.8 3.1 convolution_convert_fusion.3
  287.0 3.5 convolution_convert_fusion.2
  290.4 4.9 %all-to-all-start = ((bf16[12,128,768]{2,1,0:T(8,128)(2,1)}), bf16[12,128,768]{2,1,0:T(8,128)(2,1)}, u32[]{:S(2)}, u32[]{:S(2)}) async-start(bf16[12,128,768]{2,1,0:T(8,128)(2,1)} %bitcast.8), calls=%async_computation | async-start | bytes 4718592 | tf_op jit(solution)/shard_map/all_to_all | solution.py:1529
  296.0 12.9 %convolution_convert_fusion.1 = bf16[768,3072]{1,0:T(8,128)(2,1)} fusion(bf16[1536,768]{1,0:T(8,128)(2,1)S(1)} %copy-done.8, bf16[1536,3072]{1,0:T(8,128)(2,1)} %copy-done.2), kind=kOutput, calls=%fused_computation.28 | convolution fusion | flops 7250116608 | bytes 16515072 | tf_op jit(solution)/shard_map/dot_general | solution.py:37
  308.9 15.5 %all-to-all-done = bf16[12,128,768]{2,1,0:T(8,128)(2,1)} async-done(((bf16[12,128,768]{2,1,0:T(8,128)(2,1)}), bf16[12,128,768]{2,1,0:T(8,128)(2,1)}, u32[]{:S(2)}, u32[]{:S(2)}) %all-to-all-start) | async-done | bytes 2359328 | tf_op jit(solution)/shard_map/all_to_all | solution.py:1529
  324.4 145.4 %back.1 = (bf16[12,128,768]{2,1,0:T(8,128)(2,1)}, f32[192,2304]{1,0:T(8,128)}, f32[2,4,24,768]{3,2,1,0:T(8,128)}, f32[192,3072]{1,0:T(8,128)}, f32[2,4,96,768]{3...) custom-call(bf16[4,3,128,768]{3,2,1,0:T(8,128)(2,1)} %bitcast.75, ...), custom_call_target="tpu_custom_call" | custom-call | tf_op jit(solution)/shard_map/back/pallas_call | solution.py:1417
  469.8 0.9 slice.84
  471.4 0.8 slice_reduce_fusion.1
  474.3 3.4 copy.46
  477.7 1.4 copy.47
  479.1 1.2 copy.48
  481.1 1.4 copy.50
  482.5 1.4 copy.51
  (128 shorter events, 9.6 us)
Async XLA Ops:
  0.7 5.4 %copy-start.14 = (s32[12,12,128]{2,1,0:T(8,128)S(1)}, s32[12,12,128]{2,1,0:T(8,128)}, u32[]{:S(2)}) copy-start(s32[12,12,128]{2,1,0:T(8,128)} %param.31) | copy-start | bytes 221188
  0.7 6.8 %copy-start.24 = (bf16[192]{0:T(256)(128)(2,1)S(1)}, bf16[192]{0:T(256)(128)(2,1)}, u32[]{:S(2)}) copy-start(bf16[192]{0:T(256)(128)(2,1)} %param.19) | copy-start | bytes 1156
  0.7 6.8 %copy-start.25 = (bf16[192]{0:T(256)(128)(2,1)S(1)}, bf16[192]{0:T(256)(128)(2,1)}, u32[]{:S(2)}) copy-start(bf16[192]{0:T(256)(128)(2,1)} %param.20) | copy-start | bytes 1156
  0.7 6.8 %copy-start.26 = (bf16[192]{0:T(256)(128)(2,1)S(1)}, bf16[192]{0:T(256)(128)(2,1)}, u32[]{:S(2)}) copy-start(bf16[192]{0:T(256)(128)(2,1)} %param.22) | copy-start | bytes 1156
  0.7 6.8 %copy-start.27 = (bf16[192]{0:T(256)(128)(2,1)S(1)}, bf16[192]{0:T(256)(128)(2,1)}, u32[]{:S(2)}) copy-start(bf16[192]{0:T(256)(128)(2,1)} %param.23) | copy-start | bytes 1156
  0.7 6.8 %copy-start.28 = (bf16[192]{0:T(256)(128)(2,1)S(1)}, bf16[192]{0:T(256)(128)(2,1)}, u32[]{:S(2)}) copy-start(bf16[192]{0:T(256)(128)(2,1)} %param.24) | copy-start | bytes 1156
  0.7 6.8 %copy-start.23 = (bf16[768]{0:T(1024)(128)(2,1)S(1)}, bf16[768]{0:T(1024)(128)(2,1)}, u32[]{:S(2)}) copy-start(bf16[768]{0:T(1024)(128)(2,1)} %param.26) | copy-start | bytes 4612
  0.7 6.8 %copy-start.29 = (bf16[192]{0:T(256)(128)(2,1)S(1)}, bf16[192]{0:T(256)(128)(2,1)}, u32[]{:S(2)}) copy-start(bf16[192]{0:T(256)(128)(2,1)} %param.28) | copy-start | bytes 1156
  0.7 6.8 %copy-start.30 = (bf16[192]{0:T(256)(128)(2,1)S(1)}, bf16[192]{0:T(256)(128)(2,1)}, u32[]{:S(2)}) copy-start(bf16[192]{0:T(256)(128)(2,1)} %param.29) | copy-start | bytes 1156
  0.8 6.8 %copy-start.31 = (bf16[192]{0:T(256)(128)(2,1)S(1)}, bf16[192]{0:T(256)(128)(2,1)}, u32[]{:S(2)}) copy-start(bf16[192]{0:T(256)(128)(2,1)} %param.30) | copy-start | bytes 1156
  0.8 217.7 %all-to-all-start.1 = ((bf16[12,128,768]{2,1,0:T(8,128)(2,1)}), bf16[12,128,768]{2,1,0:T(8,128)(2,1)}, u32[]{:S(2)}, u32[]{:S(2)}) async-start(bf16[12,128,768]{2,1,0:T(8,128)(2,1)} %param.33), calls=%async_computation.1 | async-start | bytes 4718592 | tf_op jit(solution)/shard_map/all_to_all | solution.py:1529
  145.1 5.9 %copy-start.11 = (f32[1536]{0:T(1024)}, f32[1536]{0:T(1024)S(1)}, u32[]{:S(2)}) copy-start(f32[1536]{0:T(1024)S(1)} %broadcast_multiply_fusion.4) | copy-start | bytes 18436
  147.8 52.4 %copy-start.15 = (f32[1536]{0:T(1024)}, f32[1536]{0:T(1024)S(1)}, u32[]{:S(2)}) copy-start(f32[1536]{0:T(1024)S(1)} %add_rsqrt_fusion.1) | copy-start | bytes 18436
  147.9 52.3 %copy-start.17 = (f32[768]{0:T(1024)}, f32[768]{0:T(1024)S(1)}, u32[]{:S(2)}) copy-start(f32[768]{0:T(1024)S(1)} %mul.158) | copy-start | bytes 9220
  148.0 52.3 %copy-start.19 = (f32[768]{0:T(1024)}, f32[768]{0:T(1024)S(1)}, u32[]{:S(2)}) copy-start(f32[768]{0:T(1024)S(1)} %add.117) | copy-start | bytes 9220
  150.9 49.3 %copy-start.7 = (bf16[1536,768]{1,0:T(8,128)(2,1)}, bf16[1536,768]{1,0:T(8,128)(2,1)S(1)}, u32[]{:S(2)}) copy-start(bf16[1536,768]{1,0:T(8,128)(2,1)S(1)} %fusion.24) | copy-start | bytes 7077892
  151.0 49.3 %copy-start.22 = (f32[4,192]{1,0:T(4,128)S(1)}, f32[4,192]{1,0:T(4,128)}, u32[]{:S(2)}) copy-start(f32[4,192]{1,0:T(4,128)} %get-tuple-element.69) | copy-start | bytes 9220
  151.0 49.3 %copy-start.12 = (f32[1536]{0:T(1024)S(1)}, f32[1536]{0:T(1024)}, u32[]{:S(2)}) copy-start(f32[1536]{0:T(1024)} %copy-done.11) | copy-start | bytes 18436
  200.4 14.9 %copy-start.21 = (f32[4,192]{1,0:T(4,128)S(1)}, f32[4,192]{1,0:T(4,128)}, u32[]{:S(2)}) copy-start(f32[4,192]{1,0:T(4,128)} %get-tuple-element.67) | copy-start | bytes 9220
  200.4 15.0 %copy-start.20 = (f32[4,192]{1,0:T(4,128)S(1)}, f32[4,192]{1,0:T(4,128)}, u32[]{:S(2)}) copy-start(f32[4,192]{1,0:T(4,128)} %get-tuple-element.68) | copy-start | bytes 9220
  222.6 11.6 %slice-start.4 = ((s8[4718592]{0:T(1024)(128)(4,1)}), s8[4194304]{0:T(1024)(128)(4,1)S(1)}, s32[]{:S(2)}) async-start(s8[4718592]{0:T(1024)(128)(4,1)} %bitcast.92), calls=%async_computation.6 | async-start | bytes 8388608
  225.6 8.7 %slice-start.5 = ((s8[4718592]{0:T(1024)(128)(4,1)}), s8[524288]{0:T(1024)(128)(4,1)S(1)}, s32[]{:S(2)}) async-start(s8[4718592]{0:T(1024)(128)(4,1)} %bitcast.92), calls=%async_computation.7 | async-start | bytes 1048576
  225.6 24.2 %slice-start = ((s8[4718592]{0:T(1024)(128)(4,1)}), s8[4194304]{0:T(1024)(128)(4,1)S(1)}, s32[]{:S(2)}) async-start(s8[4718592]{0:T(1024)(128)(4,1)} %bitcast.68), calls=%async_computation.2 | async-start | bytes 8388608
  234.3 15.6 %slice-start.1 = ((s8[4718592]{0:T(1024)(128)(4,1)}), s8[524288]{0:T(1024)(128)(4,1)S(1)}, s32[]{:S(2)}) async-start(s8[4718592]{0:T(1024)(128)(4,1)} %bitcast.68), calls=%async_computation.3 | async-start | bytes 1048576
  234.3 15.6 %copy-start.16 = (f32[1536]{0:T(1024)S(1)}, f32[1536]{0:T(1024)}, u32[]{:S(2)}) copy-start(f32[1536]{0:T(1024)} %copy-done.15) | copy-start | bytes 18436
  234.3 15.6 %copy-start.18 = (f32[768]{0:T(1024)S(1)}, f32[768]{0:T(1024)}, u32[]{:S(2)}) copy-start(f32[768]{0:T(1024)} %copy-done.17) | copy-start | bytes 9220
  249.9 17.1 %copy-start.2 = (bf16[1536,3072]{1,0:T(8,128)(2,1)}, bf16[1536,3072]{1,0:T(8,128)(2,1)S(1)}, u32[]{:S(2)}) copy-start(bf16[1536,3072]{1,0:T(8,128)(2,1)S(1)} %fusion.8) | copy-start | bytes 28311556
  266.9 15.2 %slice-start.2 = ((s8[4718592]{0:T(1024)(128)(4,1)}), s8[524288]{0:T(1024)(128)(4,1)S(1)}, s32[]{:S(2)}) async-start(s8[4718592]{0:T(1024)(128)(4,1)} %bitcast.73), calls=%async_computation.4 | async-start | bytes 1048576
  268.7 13.3 %slice-start.3 = ((s8[4718592]{0:T(1024)(128)(4,1)}), s8[4194304]{0:T(1024)(128)(4,1)S(1)}, s32[]{:S(2)}) async-start(s8[4718592]{0:T(1024)(128)(4,1)} %bitcast.73), calls=%async_computation.5 | async-start | bytes 8388608
  290.4 5.6 %copy-start.8 = (bf16[1536,768]{1,0:T(8,128)(2,1)S(1)}, bf16[1536,768]{1,0:T(8,128)(2,1)}, u32[]{:S(2)}) copy-start(bf16[1536,768]{1,0:T(8,128)(2,1)} %copy-done.7) | copy-start | bytes 7077892
  290.4 33.9 %all-to-all-start = ((bf16[12,128,768]{2,1,0:T(8,128)(2,1)}), bf16[12,128,768]{2,1,0:T(8,128)(2,1)}, u32[]{:S(2)}, u32[]{:S(2)}) async-start(bf16[12,128,768]{2,1,0:T(8,128)(2,1)} %bitcast.8), calls=%async_computation | async-start | bytes 4718592 | tf_op jit(solution)/shard_map/all_to_all | solution.py:1529
  469.8 7.8 %copy-start.6 = (bf16[12,128,768]{2,1,0:T(8,128)(2,1)S(1)}, bf16[12,128,768]{2,1,0:T(8,128)(2,1)}, u32[]{:S(2)}) copy-start(bf16[12,128,768]{2,1,0:T(8,128)(2,1)} %get-tuple-element.111) | copy-start | bytes 7077892
  (12 other events, 38.7 us)

commit v3 on v2

--- a/solution.py
+++ b/solution.py
@@ -453,7 +453,7 @@
     return pl.multiple_of(value, by)
 
 
-def attend_kernel(
+def forward_kernel(
     chips,
     depth,
     heads,
@@ -464,6 +464,7 @@
     ow_ref,
     ew_ref,
     rw_ref,
+    cot_ref,
     x_out,
     ctx_out,
     q_out,
@@ -476,18 +477,32 @@
     ow_out,
     ew_out,
     rw_out,
+    n1_out,
+    inv_out,
+    ml_out,
+    hid_out,
+    slope_out,
+    lo_out,
+    gr_out,
+    gb_out,
+    sum_out,
     xbuf,
     posbuf,
     wbuf,
     vbuf,
     bias,
-    qkv,
-    qs,
-    ks,
-    vs,
-    ps,
-    os,
     ctxb,
+    ctxt,
+    owbuf,
+    ewbuf,
+    rwbuf,
+    cbuf,
+    n1buf,
+    invbuf,
+    mlbuf,
+    vecs,
+    upb,
+    sums,
     tok_s,
     tok_r,
     tokc_s,
@@ -510,8 +525,14 @@
     wc_r,
     ctx_s,
     ctx_r,
+    cot_s,
+    cot_r,
+    oc_s,
+    oc_r,
     loc,
     out_sem,
+    slope_sem,
+    att_sem,
 ):
     me = Place(chips, depth)
     z, chip, core = me.z, me.chip, me.core
@@ -578,42 +599,37 @@
             aw_ref.at[:, pl.ds(multiple(part * 2 * half + core * half, 128), half)],
             wbuf.at[pl.ds(multiple(z * rows_z, 8), rows_z), pl.ds(part * half, half)],
         )
-    eighth = ow_ref.shape[0] // (2 * chips)
     wide = ew_ref.shape[1] // (2 * chips)
     tall = rw_ref.shape[0] // (2 * chips)
-
-    def piece(ref, kind, at):
+    mid_rows = rows_z // 2
+    mine_at = core * chips + chip
+
+    def piece(kind):
         if kind == 0:
-            return ref.at[pl.ds(multiple(at * eighth, 8), eighth)]
+            return ow_ref.at[pl.ds(multiple(core * mid_rows, 8), mid_rows)]
         if kind == 1:
-            return ref.at[:, pl.ds(multiple(at * wide, 128), wide)]
-        return ref.at[pl.ds(multiple(at * tall, 8), tall)]
-
-    shards = (ow_ref, ew_ref, rw_ref)
-    fulls = (ow_out, ew_out, rw_out)
-    mine_at = core * chips + chip
-
-    def place(kind, zz, at):
+            return ew_ref.at[:, pl.ds(multiple(mine_at * wide, 128), wide)]
+        return rw_ref.at[pl.ds(multiple(mine_at * tall, 8), tall)]
+
+    def place(kind, zz):
         if kind == 0:
-            return ow_out.at[zz, at]
+            return owbuf.at[zz, core]
         if kind == 1:
-            return ew_out.at[zz, :, pl.ds(multiple(at * wide, 128), wide)]
-        return rw_out.at[zz, at]
+            return ewbuf.at[zz, :, pl.ds(multiple(mine_at * wide, 128), wide)]
+        return rwbuf.at[zz, mine_at]
 
     def place_all(kind, at):
-        if kind == 0:
-            return ow_out.at[:, at]
         if kind == 1:
-            return ew_out.at[:, :, pl.ds(multiple(at * wide, 128), wide)]
-        return rw_out.at[:, at]
+            return ewbuf.at[:, :, pl.ds(multiple(at * wide, 128), wide)]
+        return rwbuf.at[:, at]
 
     for kind in range(3):
-        keep(piece(shards[kind], kind, mine_at), place(kind, z, mine_at))
+        keep(piece(kind), place(kind, z))
 
     def wz_copy(kind, k):
         return far_copy(
-            piece(shards[kind], kind, mine_at),
-            place(kind, z, mine_at),
+            piece(kind),
+            place(kind, z),
             (wz_s, wz_r),
             kind * (depth - 1) + k - 1,
             me.tower(k),
@@ -625,7 +641,7 @@
             place_all(kind, at),
             place_all(kind, at),
             (wp_s, wp_r),
-            kind * (chips - 1) + k - 1,
+            (kind - 1) * (chips - 1) + k - 1,
             me.plane(k),
         )
 
@@ -635,9 +651,20 @@
             place_all(kind, at),
             place_all(kind, at),
             (wc_s, wc_r),
-            kind * chips + origin_k,
+            (kind - 1) * chips + origin_k,
             me.sibling(),
         )
+
+    def oc_copy():
+        spot = owbuf.at[:, core]
+        return far_copy(spot, spot, (oc_s, oc_r), 0, me.sibling())
+
+    def cot_copy(k):
+        return far_copy(
+            mine(cot_ref, me.chip_at(k)), cbuf.at[chip], (cot_s, cot_r), k - 1, me.plane(k)
+        )
+
+    keep(mine(cot_ref, chip), cbuf.at[chip])
 
     for copy in local[:2]:
         copy.wait()
@@ -661,21 +688,24 @@
         for copy in (posc_copy(k), tokc_copy(k)):
             copy.start()
             sends.append(copy)
+    for k in range(1, chips):
+        cot_copy(k).start()
+        sends.append(cot_copy(k))
     for copy in local[2:6]:
         copy.wait()
     for k in range(1, depth):
         vec_copy(k).wait_recv()
         for part in range(3):
             aw_copy(k, part).wait_recv()
+    for k in range(1, depth):
+        wz_copy(1, k).start()
+        for kind in range(3):
+            sends.append(wz_copy(kind, k))
     for k in range(chips):
         posc_copy(k).wait_recv()
         tokc_copy(k).wait_recv()
     for copy in local[6:]:
         copy.wait()
-    for kind in range(3):
-        for k in range(1, depth):
-            sends.append(wz_copy(kind, k))
-            sends[-1].start()
 
     outs = []
 
@@ -706,18 +736,20 @@
     bias[0, 0:1, half : 2 * half] = jnp.zeros((1, half), f32)
     bias[1, 0:1, half : 2 * half] = jnp.zeros((1, half), f32)
     added = bias[core, 0:1, :]
+    for zz in range(depth):
+        for row in range(8):
+            vecs[row : row + 1, zz * quarter : (zz + 1) * quarter] = vbuf[
+                zz, row : row + 1, :quarter
+            ]
+        steps = upb.shape[1] // (depth * quarter)
+        for row in range(steps):
+            to = (zz * steps + row) * quarter
+            upb[0:1, to : to + quarter] = vbuf[zz, 8 + row : 9 + row, :quarter]
 
     cluster = tok_ref.shape[1]
     blocks = 2 * chips
     share = cluster // blocks
     width = tok_ref.shape[2]
-
-    @pl.loop(0, blocks)
-    def _(jj):
-        x = xbuf[lax.div(jj, chips), lax.rem(jj, chips)].reshape(per * cluster, width)
-        mixed = (dot_rows(x, wbuf[...]) + added).astype(bf16)
-        for at in range(3 * pairs):
-            qkv[at, jj] = mixed[:, at * 128 : (at + 1) * 128].reshape(per, cluster, 128)
 
     slots = lax.broadcasted_iota(jnp.int32, (cluster, cluster), 0)
     low = lax.broadcasted_iota(jnp.int32, (cluster, 128), 1) < size
@@ -731,93 +763,245 @@
         ]
         return rows
 
-    def weights_step(stage):
-        if stage == 0:
-            for kind in range(3):
-                for k in range(1, depth):
-                    wz_copy(kind, k).wait_recv()
-                for k in range(1, chips):
-                    wp_copy(kind, k, chip).start()
-                wc_copy(kind, 0).start()
-
-    @pl.loop(0, per)
-    def _(i):
-        @pl.loop(0, pairs)
-        def _(pair):
-            at = i * pairs + pair
-            for jj in range(blocks):
-                tq = jnp.concatenate(tables(jj, i, pair, 0), axis=1)
-                tk = jnp.concatenate(tables(jj, i, pair, 1), axis=1)
-                q = stack_lanes(qkv[pair, jj, i], low)
-                k = stack_lanes(qkv[pairs + pair, jj, i], low)
-                v = stack_lanes(qkv[2 * pairs + pair, jj, i], low)
-                span = slice(jj * share, (jj + 1) * share)
-                sq = dot_rows(tq, q).astype(bf16)
-                skv = dot_rows(tk, jnp.concatenate([k, v], axis=1)).astype(bf16)
-                qs[at, :, span, :] = sq.reshape(blocks, share, 128)
-                ks[at, :, span, :] = skv[:, :128].reshape(blocks, share, 128)
-                vs[at, :, span, :] = skv[:, 128:].reshape(blocks, share, 128)
-            for c in range(blocks):
-                scores = dot_lanes(qs[at, c], stack_lanes(ks[at, c], low)) * scale
-                halves = []
-                for h in range(2):
-                    s = scores[:, h * cluster : (h + 1) * cluster]
-                    e = jnp.exp(s - jnp.max(s, axis=1, keepdims=True))
-                    halves.append((e / jnp.sum(e, axis=1, keepdims=True)).astype(bf16))
-                probs = jnp.concatenate(halves, axis=1)
-                ps[at, c] = probs
-                o = dot_rows(probs, stack_lanes(vs[at, c], low)).astype(bf16)
-                os[c] = o
-            for jj in range(blocks):
-                tq = jnp.concatenate(tables(jj, i, pair, 0), axis=0)
-                rows = os[:, jj * share : (jj + 1) * share, :].reshape(cluster, 128)
-                back = dot_first(tq, stack_lanes(rows, low)).astype(bf16)
-                ctxb[jj // chips, jj % chips, i, :, pl.ds(multiple(pair * 128, 128), 128)] = back
-
-        @pl.when(i == 0)
+    def plane_stage(kind):
+        for k in range(1, depth):
+            wz_copy(kind, k).wait_recv()
+        for k in range(1, chips):
+            wp_copy(kind, k, chip).start()
+        wc_copy(kind, 0).start()
+
+    def hook(i, pair):
+        @pl.when((i == 0) & (pair == 0))
         def _():
-            weights_step(0)
-
-    far = far_copy(
-        ctxb.at[1 - core],
-        ctx_out.at[:, :, :, pl.ds(multiple(core * half, 128), half)],
-        (ctx_s, ctx_r),
-        0,
-        me.sibling(),
-    )
-    far.start()
-    emit(ctxb.at[core], ctx_out.at[:, :, :, pl.ds(multiple(core * half, 128), half)])
-    emit(qs, q_out)
-    emit(ks, k_out)
-    emit(vs, v_out)
-    emit(ps, p_out)
-    for kind in range(3):
+            plane_stage(1)
+            for k in range(1, depth):
+                wz_copy(2, k).start()
+            for k in range(1, depth):
+                wz_copy(0, k).start()
+
+        @pl.when((i == min(1, per - 1)) & (pair == pairs - 1))
+        def _():
+            plane_stage(2)
+            for k in range(1, depth):
+                wz_copy(0, k).wait_recv()
+            oc_copy().start()
+
+    def attention(qkv, qs, ks, vs, ps, os):
+        @pl.loop(0, blocks)
+        def _(jj):
+            x = xbuf[lax.div(jj, chips), lax.rem(jj, chips)].reshape(per * cluster, width)
+            mixed = (dot_rows(x, wbuf[...]) + added).astype(bf16)
+            for at in range(3 * pairs):
+                qkv[at, jj] = mixed[:, at * 128 : (at + 1) * 128].reshape(per, cluster, 128)
+
+        @pl.loop(0, per)
+        def _(i):
+            @pl.loop(0, pairs)
+            def _(pair):
+                at = i * pairs + pair
+                for jj in range(blocks):
+                    tq = jnp.concatenate(tables(jj, i, pair, 0), axis=1)
+                    tk = jnp.concatenate(tables(jj, i, pair, 1), axis=1)
+                    q = stack_lanes(qkv[pair, jj, i], low)
+                    k = stack_lanes(qkv[pairs + pair, jj, i], low)
+                    v = stack_lanes(qkv[2 * pairs + pair, jj, i], low)
+                    span = slice(jj * share, (jj + 1) * share)
+                    sq = dot_rows(tq, q).astype(bf16)
+                    skv = dot_rows(tk, jnp.concatenate([k, v], axis=1)).astype(bf16)
+                    qs[at, :, span, :] = sq.reshape(blocks, share, 128)
+                    ks[at, :, span, :] = skv[:, :128].reshape(blocks, share, 128)
+                    vs[at, :, span, :] = skv[:, 128:].reshape(blocks, share, 128)
+                for c in range(blocks):
+                    scores = dot_lanes(qs[at, c], stack_lanes(ks[at, c], low)) * scale
+                    halves = []
+                    for h in range(2):
+                        s = scores[:, h * cluster : (h + 1) * cluster]
+                        e = jnp.exp(s - jnp.max(s, axis=1, keepdims=True))
+                        halves.append((e / jnp.sum(e, axis=1, keepdims=True)).astype(bf16))
+                    probs = jnp.concatenate(halves, axis=1)
+                    ps[at, c] = probs
+                    o = dot_rows(probs, stack_lanes(vs[at, c], low)).astype(bf16)
+                    os[c] = o
+                for jj in range(blocks):
+                    tq = jnp.concatenate(tables(jj, i, pair, 0), axis=0)
+                    rows = os[:, jj * share : (jj + 1) * share, :].reshape(cluster, 128)
+                    back = dot_first(tq, stack_lanes(rows, low)).astype(bf16)
+                    ctxb[jj // chips, jj % chips, i, :, pl.ds(multiple(pair * 128, 128), 128)] = back
+                hook(i, pair)
+
+        pieces = ((qs, q_out), (ks, k_out), (vs, v_out), (ps, p_out))
+        copies = [
+            pltpu.make_async_copy(src, dst, att_sem.at[n]) for n, (src, dst) in enumerate(pieces)
+        ]
+        far, own = ctx_copies()
+        for copy in copies + [far, own]:
+            copy.start()
+        for copy in copies + [far, own]:
+            copy.wait()
+
+    def ctx_copies():
+        lanes = pl.ds(multiple(core * half, 128), half)
+        far = far_copy(
+            ctxb.at[1 - core], ctxt.at[:, :, :, lanes], (ctx_s, ctx_r), 0, me.sibling()
+        )
+        own = pltpu.make_async_copy(ctxb.at[core], ctxt.at[:, :, :, lanes], att_sem.at[4])
+        return far, own
+
+    group = (per * pairs, blocks, cluster, 128)
+    pl.run_scoped(
+        attention,
+        pltpu.VMEM((3 * pairs, blocks, per, cluster, 128), bf16),
+        pltpu.VMEM(group, bf16),
+        pltpu.VMEM(group, bf16),
+        pltpu.VMEM(group, bf16),
+        pltpu.VMEM((per * pairs, blocks, cluster, 2 * cluster), bf16),
+        pltpu.VMEM((blocks, cluster, 128), bf16),
+    )
+
+    def from_plane(kind):
         for k in range(1, chips):
             wp_copy(kind, k, me.chip_at(-k)).wait_recv()
             wc_copy(kind, chips - k).start()
-    for kind in range(3):
+
+    def from_sibling(kind):
         for k in range(chips):
             wc_copy(kind, k).wait()
         for k in range(1, chips):
             wp_copy(kind, k, chip).wait_send()
-    far.wait()
-    awc.wait_recv()
-    for copy in sends:
-        copy.wait_send()
-    for copy in outs:
-        copy.wait()
-
-
-def attend(tokens, pos, attend_weight, vectors, output_weight, expand_weight, reduce_weight, chips, depth, heads):
+
+    oc_copy().wait()
+    from_plane(1)
+    from_sibling(1)
+    emit(ctxt, ctx_out)
+    emit(owbuf, ow_out)
+    emit(ewbuf, ew_out)
+    tile = per * cluster
+    hidden = upb.shape[1]
+    eps = epsilon
+
+    def moments(rows):
+        center = jnp.mean(rows, axis=1, keepdims=True)
+        centered = rows - center
+        spread = jnp.mean(centered * centered, axis=1, keepdims=True)
+        inverse = lax.rsqrt(spread + eps)
+        return centered * inverse, inverse
+
+    def slope_out_copy(j, slot):
+        return pltpu.make_async_copy(sbuf.at[slot], slope_out.at[j], slope_sem.at[slot])
+
+    def vec(row):
+        return vecs[row : row + 1, :]
+
+    def feed(hbuf, sbuf):
+        def slope_copy(j, slot):
+            return pltpu.make_async_copy(sbuf.at[slot], slope_out.at[j], slope_sem.at[slot])
+
+        @pl.loop(0, chips)
+        def _(j):
+            slot = lax.rem(j, 2)
+
+            @pl.when(j >= 2)
+            def _():
+                slope_copy(j - 2, slot).wait()
+
+            rows = ctxt[j].reshape(tile, width)
+            branch = dot_rows(rows, owbuf[...].reshape(width, width))
+            resid = xbuf[core, j].reshape(tile, width).astype(f32) + branch + vec(2)
+            normed, inverse = moments(resid)
+            n1buf[j] = normed
+            invbuf[j] = jnp.broadcast_to(inverse, (tile, 128))
+            mlbuf[j] = (normed * vec(3) + vec(4)).astype(bf16)
+
+            @pl.loop(0, hidden // 384)
+            def _(n):
+                lanes = pl.ds(multiple(n * 384, 128), 384)
+                weight = ewbuf[:, :, lanes].reshape(width, 384)
+                pre = dot_rows(mlbuf[j], weight) + upb[0:1, lanes]
+                cumulative = 0.5 * (1.0 + lax.erf(pre * 0.5**0.5))
+                density = jnp.exp(-0.5 * pre * pre) * (2.0 * math.pi) ** (-0.5)
+                hbuf[j, :, lanes] = (pre * cumulative).astype(bf16)
+                sbuf[slot, :, lanes] = (cumulative + pre * density).astype(bf16)
+
+            slope_copy(j, slot).start()
+
+        emit(n1buf, n1_out)
+        emit(invbuf, inv_out)
+        emit(mlbuf, ml_out)
+        emit(hbuf, hid_out)
+        from_plane(2)
+        from_sibling(2)
+        emit(rwbuf, rw_out)
+        for copy in sends:
+            copy.wait_send()
+        for k in range(1, chips):
+            cot_copy(k).wait_recv()
+        for j in range(max(chips - 2, 0), chips):
+            slope_copy(j, j % 2).wait()
+        for copy in outs:
+            copy.wait()
+        sums[...] = jnp.zeros_like(sums)
+
+        @pl.loop(0, chips)
+        def _(j):
+            branch = vec(5)
+            for zz in range(depth):
+                span = hidden // depth
+                branch = branch + dot_rows(
+                    hbuf[j, :, zz * span : (zz + 1) * span], rwbuf[zz].reshape(span, width)
+                )
+            middle = n1buf[j] * vec(3) + vec(4)
+            normed, inverse = moments(middle + branch)
+            upstream = cbuf[j].reshape(tile, width).astype(f32)
+            cbuf[j] = (normed * vec(6) + vec(7)).astype(bf16).reshape(per, cluster, width)
+            sums[0:1, :] += jnp.sum(upstream * normed, axis=0, keepdims=True)
+            sums[1:2, :] += jnp.sum(upstream, axis=0, keepdims=True)
+            scaled = upstream * vec(6)
+            first = jnp.mean(scaled, axis=1, keepdims=True)
+            second = jnp.mean(scaled * normed, axis=1, keepdims=True)
+            grad = inverse * (scaled - first - normed * second)
+            n1buf[j] = grad
+            low_grad = grad.astype(bf16)
+            sums[2:3, :] += jnp.sum(low_grad.astype(f32), axis=0, keepdims=True)
+            ctxt[j] = low_grad.reshape(per, cluster, width)
+
+        done = len(outs)
+        emit(cbuf, lo_out)
+        emit(n1buf, gr_out)
+        emit(ctxt, gb_out)
+        emit(sums, sum_out)
+        awc.wait_recv()
+        for copy in outs[done:]:
+            copy.wait()
+
+    pl.run_scoped(
+        feed,
+        pltpu.VMEM((chips, tile, hidden), bf16),
+        pltpu.VMEM((2, tile, hidden), bf16),
+    )
+
+
+def forward(
+    tokens,
+    pos,
+    attend_weight,
+    vectors,
+    output_weight,
+    expand_weight,
+    reduce_weight,
+    cotangent,
+    chips,
+    depth,
+    heads,
+):
     seqs, cluster, width = tokens.shape
     per, blocks, pairs = seqs // chips, 2 * chips, heads // 4
     half = width // 2
     rows_z = attend_weight.shape[0]
-    wide = expand_weight.shape[1]
+    hidden = expand_weight.shape[1]
     items = per * pairs
+    tile = per * cluster
     dma = pltpu.SemaphoreType.DMA
     anywhere = pl.BlockSpec(memory_space=pl.ANY)
-    eighth = output_weight.shape[0] // blocks
     tall = reduce_weight.shape[0] // blocks
     shapes = [
         ((2, chips, per, cluster, width), bf16),
@@ -829,44 +1013,70 @@
         ((2, chips, per, 2 * heads, cluster), jnp.int32),
         ((2, depth * rows_z, 3 * half), bf16),
         ((depth,) + vectors.shape, f32),
-        ((depth, blocks, eighth, width), bf16),
-        ((depth, rows_z, wide), bf16),
+        ((depth, 2, rows_z // 2, width), bf16),
+        ((depth, rows_z, hidden), bf16),
         ((depth, blocks, tall, width), bf16),
+        ((chips, tile, width), f32),
+        ((chips, tile, 128), f32),
+        ((chips, tile, width), bf16),
+        ((chips, tile, hidden), bf16),
+        ((chips, tile, hidden), bf16),
+        ((chips, per, cluster, width), bf16),
+        ((chips, tile, width), f32),
+        ((chips, per, cluster, width), bf16),
+        ((8, width), f32),
     ]
     t, c = depth - 1, chips - 1
+    vm = pltpu.VMEM
     return pl.pallas_call(
-        functools.partial(attend_kernel, chips, depth, heads),
+        functools.partial(forward_kernel, chips, depth, heads),
         out_shape=[jax.ShapeDtypeStruct(*s) for s in shapes],
-        in_specs=[anywhere] * 7,
+        in_specs=[anywhere] * 8,
         out_specs=[anywhere] * len(shapes),
         scratch_shapes=[
-            pltpu.VMEM(shapes[0][0], bf16),
-            pltpu.VMEM(shapes[6][0], jnp.int32),
-            pltpu.VMEM(shapes[7][0][1:], bf16),
-            pltpu.VMEM(shapes[8][0], f32),
-            pltpu.VMEM((2, 8, 3 * half), f32),
-            pltpu.VMEM((3 * pairs, blocks, per, cluster, 128), bf16),
-            pltpu.VMEM(shapes[2][0], bf16),
-            pltpu.VMEM(shapes[3][0], bf16),
-            pltpu.VMEM(shapes[4][0], bf16),
-            pltpu.VMEM(shapes[5][0], bf16),
-            pltpu.VMEM((blocks, cluster, 128), bf16),
-            pltpu.VMEM((2, chips, per, cluster, half), bf16),
+            vm(shapes[0][0], bf16),
+            vm(shapes[6][0], jnp.int32),
+            vm(shapes[7][0][1:], bf16),
+            vm(shapes[8][0], f32),
+            vm((2, 8, 3 * half), f32),
+            vm((2, chips, per, cluster, half), bf16),
+            vm(shapes[1][0], bf16),
+            vm(shapes[9][0], bf16),
+            vm(shapes[10][0], bf16),
+            vm(shapes[11][0], bf16),
+            vm(shapes[17][0], bf16),
+            vm(shapes[12][0], f32),
+            vm(shapes[13][0], f32),
+            vm(shapes[14][0], bf16),
+            vm((8, width), f32),
+            vm((8, hidden), f32),
+            vm((8, width), f32),
             dma((c,)), dma((c,)), dma((chips,)), dma((chips,)),
             dma((c,)), dma((c,)), dma((chips,)), dma((chips,)),
             dma((3 * t,)), dma((3 * t,)), dma((1,)), dma((1,)),
             dma((t,)), dma((t,)),
             dma((3 * t,)), dma((3 * t,)),
-            dma((3 * c,)), dma((3 * c,)),
-            dma((3 * chips,)), dma((3 * chips,)),
+            dma((2 * c,)), dma((2 * c,)),
+            dma((2 * chips,)), dma((2 * chips,)),
             dma((1,)), dma((1,)),
-            dma((9,)), dma((9,)),
+            dma((c,)), dma((c,)),
+            dma((1,)), dma((1,)),
+            dma((12,)), dma((24,)), dma((2,)), dma((5,)),
         ],
         compiler_params=pltpu.CompilerParams(
-            collective_id=1, has_side_effects=True, vmem_limit_bytes=60 * 2**20
+            collective_id=1, has_side_effects=True, vmem_limit_bytes=63 * 2**20
         ),
-        name="attend",
-    )(tokens, pos, attend_weight, vectors, output_weight, expand_weight, reduce_weight)
+        name="forward",
+    )(
+        tokens,
+        pos,
+        attend_weight,
+        vectors,
+        output_weight,
+        expand_weight,
+        reduce_weight,
+        cotangent,
+    )
 
 
 def add_into(target, at, parts):
@@ -1550,34 +1760,58 @@
     )
     count = small.shape[0] // quarter
     vectors = jnp.pad(small.reshape(count, quarter), ((0, 16 - count), (0, 256 - quarter)))
-    (x_all, context, qs, ks, vs, ps, pos_all, attend_all, vec_all, out_all, exp_all, red_all) = attend(
-        tokens, pos, attend_weight, vectors, output_weight, expand_weight, reduce_weight, chips, depth, heads
+    (
+        x_all,
+        context,
+        qs,
+        ks,
+        vs,
+        ps,
+        pos_all,
+        attend_all,
+        vec_all,
+        out_all,
+        exp_all,
+        red_all,
+        normed_one,
+        inverse_one,
+        middle_low,
+        hidden,
+        slope,
+        layer_out,
+        grad_resid_two,
+        grad_branch_two,
+        late_sums,
+    ) = forward(
+        tokens,
+        pos,
+        attend_weight,
+        vectors,
+        output_weight,
+        expand_weight,
+        reduce_weight,
+        cotangent,
+        chips,
+        depth,
+        heads,
     )
     full = jnp.transpose(vec_all[:, :8, :quarter], (1, 0, 2)).reshape(8, width)
-    bias_up = vec_all[:, 8:count, :quarter].reshape(-1)
     output_full = out_all.reshape(width, width)
     expand_full = exp_all.reshape(width, -1)
     reduce_full = red_all.reshape(-1, width)
-    mine = lax.dynamic_index_in_dim(x_all, core, 0, keepdims=False).reshape(rows, width)
     context = context.reshape(rows, width)
-    resid_one = mine.astype(f32) + jnp.dot(context, output_full, preferred_element_type=f32) + full[2]
-    middle, normed_one, inverse_one = layer_norm(resid_one, full[3], full[4])
-    middle_low = lax.optimization_barrier(middle.astype(bf16))
-    pre = jnp.dot(middle_low, expand_full, preferred_element_type=f32) + bias_up
-    hidden = jax.nn.gelu(pre, approximate=False).astype(bf16)
-    hidden = lax.optimization_barrier(hidden)
-    resid_two = middle + jnp.dot(hidden, reduce_full, preferred_element_type=f32) + full[5]
-    final, normed_two, inverse_two = layer_norm(resid_two, full[6], full[7])
-    layer_out = swap(final.astype(bf16).reshape(seqs, cluster, width))
-    upstream = swap(cotangent).reshape(rows, width).astype(f32)
-    grad_second_gain = jnp.sum(upstream * normed_two, axis=0)
-    grad_second_shift = jnp.sum(upstream, axis=0)
-    grad_resid_two = norm_back(upstream, normed_two, inverse_two, full[6])
-    grad_branch_two = grad_resid_two.astype(bf16)
-    grad_reduce_bias = jnp.sum(grad_branch_two, axis=0, dtype=f32)
+    normed_one = normed_one.reshape(rows, width)
+    inverse_one = inverse_one.reshape(rows, 128)[:, :1]
+    middle_low = middle_low.reshape(rows, width)
+    hidden = hidden.reshape(rows, -1)
+    slope = slope.reshape(rows, -1)
+    grad_resid_two = grad_resid_two.reshape(rows, width)
+    grad_branch_two = grad_branch_two.reshape(rows, width)
+    layer_out = swap(layer_out.reshape(seqs, cluster, width))
+    grad_second_gain, grad_second_shift, grad_reduce_bias = late_sums[0], late_sums[1], late_sums[2]
     grad_reduce = transpose_left(hidden, grad_branch_two)
     grad_hidden = transpose_right(grad_branch_two, reduce_full)
-    grad_pre = (grad_hidden * gelu_slope(pre)).astype(bf16)
+    grad_pre = (grad_hidden * slope.astype(f32)).astype(bf16)
     grad_pre = lax.optimization_barrier(grad_pre)
     grad_expand_bias = jnp.sum(grad_pre, axis=0, dtype=f32)
     grad_expand = transpose_left(middle_low, grad_pre)

time: 493 us -> 392 us (0.80)
  matrix products: 132 us -> 57.5 us
  other arithmetic: 25.1 us -> 7.54 us
  Pallas kernels: 275 us -> 291 us
  waiting for transfers between devices: 15.5 us -> 0.01 us
  starting transfers between devices: 10.2 us -> 4.95 us
    dot_general x3 -> x0, matrix products: 66.4 us -> none  [the longest x1 49.2 us: per_chip(): pre = jnp.dot(middle_low, expand_full, preferred_element_type=f32) + bias_up]
    pallas_call x1, Pallas kernels: 130 us -> 148 us  [forward(): pl.pallas_call(functools.partial(forward_kernel, chips, depth, heads), ou...]
    reduce_sum x5 -> x0, other arithmetic: 17.3 us -> none  [the longest x1 6.54 us: per_chip(): grad_reduce_bias = jnp.sum(grad_branch_two, axis=0, dtype=f32)]
    all_to_all x2 -> x1, waiting for transfers between devices: 15.5 us -> 0.01 us  [swap(): lax.all_to_all(x, 'seq', split_axis=0, concat_axis=0, tiled=True, axis_in...]
    dot_general x3, matrix products: 36 us -> 29 us  [transpose_right(): lax.dot_general(first, second, (((1,), (1,)), ((), ())), preferred_elemen...]
    concatenate x1, local copies, waits for them, and re-layouts: 0.09 us -> 6.11 us  [per_chip(): jnp.concatenate([v.astype(f32) for v in (query_bias, value_bias, output_b...]
    all_to_all x2 -> x1, starting transfers between devices: 10.2 us -> 4.95 us  [swap(): lax.all_to_all(x, 'seq', split_axis=0, concat_axis=0, tiled=True, axis_in...]
    unnamed x96 -> x38, local copies, waits for them, and re-layouts: 14.3 us -> 11.4 us
  transfers between devices with their start and end apart: 2 -> 1, of which waited for: 1 -> 0; matrix products, arithmetic and copies ran while one was open for 19% -> 17% of each run, Pallas kernels for 27% -> 0%
where the time goes in v3:
time: 392 us; the launch traced here: 386 us
  Pallas kernels  291 us (74%)
  matrix products  57.5 us (15%)
  local copies, waits for them, and re-layouts  23.9 us (6%)
  other arithmetic  7.54 us (2%)
  starting transfers between devices  4.95 us (1%)
    pallas_call x1, Pallas kernels, forward(): pl.pallas_call(functools.partial(forward_kernel, chips, depth, heads), ou...  148 us
    pallas_call x1, Pallas kernels, back(): pl.pallas_call(functools.partial(back_kernel, chips, depth, heads), out_s...  142 us
    dot_general x3, matrix products, transpose_right(): lax.dot_general(first, second, (((1,), (1,)), ((), ())), preferred_elemen...  29 us
    dot_general x3, matrix products, transpose_left(): lax.dot_general(first, second, (((0,), (0,)), ((), ())), preferred_elemen...  27.9 us
    unnamed x38, local copies, waits for them, and re-layouts  11.4 us
  transfers between devices with their start and end apart: 1, of which 0 were waited for; matrix products, arithmetic and copies ran while one was open for 17% of the time, Pallas kernels for 0%

profile of v3, /device:TPU:0, one launch (start us, length us, event | category | flops | bytes accessed | tf_op | source)
XLA Modules:
  0.0 385.7 jit_solution(15824577875054163020)
XLA Ops:
  0.7 6.1 %concatenate.32 = bf16[2304]{0:T(1024)(128)(2,1)S(1)} concatenate(bf16[192]{0:T(256)(128)(2,1)} %param.19, bf16[192]{0:T(256)(128)(2,1)} %param.20, bf16[192]{0:T(256)(128)(2,1)} %param.22, bf16[192]{0:T(256)(128)(2,1)} %param.23, bf16[192]{0:T(256)(128)(2,1)} %param.24, bf16[192]{0:T(256)(128)(2,1)} %param.28, bf16[192]{0:T(256)(128)(2,1)} %param.29, bf16[192]{0:T(256)(128)(2,1)} %param.30, ...), dimensions={0} | concatenate | bytes 9216 | tf_op jit(solution)/shard_map/concatenate | solution.py:1745
  6.9 0.6 pad_convert_fusion.vec_ref
  7.5 1.0 add_select_fusion
  8.5 0.6 fusion.6
  9.1 0.7 convert_element_type.64.pos_ref
  9.8 148.1 %forward.1 = (bf16[2,4,3,128,768]{4,3,2,1,0:T(8,128)(2,1)}, bf16[4,3,128,768]{3,2,1,0:T(8,128)(2,1)}, bf16[9,8,128,128]{3,2,1,0:T(8,128)(2,1)}, bf16[9,8,128,128...) custom-call(bf16[12,128,768]{2,1,0:T(8,128)(2,1)} %tok_ref.1, ...), custom_call_target="tpu_custom_call" | custom-call | tf_op jit(solution)/shard_map/forward/pallas_call | solution.py:1031
  158.0 4.9 %all-to-all-start = ((bf16[12,128,768]{2,1,0:T(8,128)(2,1)}), bf16[12,128,768]{2,1,0:T(8,128)(2,1)}, u32[]{:S(2)}, u32[]{:S(2)}) async-start(bf16[12,128,768]{2,1,0:T(8,128)(2,1)} %bitcast.71), calls=%async_computation | async-start | bytes 4718592 | tf_op jit(solution)/shard_map/all_to_all | solution.py:1739
  163.0 0.3 slice_reduce_fusion
  163.2 0.9 slice_reduce_fusion.4
  164.3 12.5 %convolution_convert_fusion = bf16[3072,768]{1,0:T(8,128)(2,1)} fusion(bf16[1536,3072]{1,0:T(8,128)(2,1)} %bitcast.86, bf16[1536,768]{1,0:T(8,128)(2,1)} %bitcast.91), kind=kOutput, calls=%fused_computation.3 | convolution fusion | flops 7250116608 | bytes 16515072 | tf_op jit(solution)/shard_map/dot_general | solution.py:37
  176.7 11.6 %fusion = bf16[1536,3072]{1,0:T(8,128)(2,1)S(1)} fusion(bf16[1536,3072]{1,0:T(8,128)(2,1)} %bitcast.85, bf16[1536,768]{1,0:T(8,128)(2,1)} %bitcast.92, bf16[3072,768]{1,0:T(8,128)(2,1)} %bitcast.88), kind=kOutput, calls=%fused_computation.1 | convolution fusion | flops 7261913088 | bytes 25952256 | tf_op jit(solution)/shard_map/dot_general | solution.py:43
  188.4 1.9 convert_reduce_fusion
  190.2 1.7 copy-done.1
  192.0 13.9 %fusion.4 = (f32[768]{0:T(1024)S(1)}, f32[1536]{0:T(1024)S(1)}, f32[1536]{0:T(1024)S(1)}, f32[768]{0:T(1024)S(1)}, f32[1536,768]{1,0:T(8,128)}) fusion(f32[4,384,768]{2,1,0:T(8,128)S(1)} %bitcast.69, f32[768]{0:T(1024)S(1)} %mul.60, bf16[1536,3072]{1,0:T(8,128)(2,1)S(1)} %fusion, bf16[768,3072]{1,0:T(8,128)(2,1)} %bitcast.87, ...), kind=kOutput, calls=%fused_computation.11 | convolution fusion | flops 7257189376 | bytes 28333056 | tf_op jit(solution)/shard_map/dot_general | solution.py:43
  205.9 3.3 convert_reduce_fusion.1
  209.3 3.1 convolution_convert_fusion.3
  212.4 3.5 convolution_convert_fusion.2
  216.0 0.6 pad_bitcast_fusion.gv_ref
  216.6 12.3 %convolution_convert_fusion.1 = bf16[768,3072]{1,0:T(8,128)(2,1)} fusion(bf16[1536,768]{1,0:T(8,128)(2,1)} %bitcast.89, bf16[1536,3072]{1,0:T(8,128)(2,1)} %copy-done.1), kind=kOutput, calls=%fused_computation.4 | convolution fusion | flops 7250116608 | bytes 16515072 | tf_op jit(solution)/shard_map/dot_general | solution.py:37
  228.9 142.5 %back.1 = (bf16[12,128,768]{2,1,0:T(8,128)(2,1)}, f32[192,2304]{1,0:T(8,128)}, f32[2,4,24,768]{3,2,1,0:T(8,128)}, f32[192,3072]{1,0:T(8,128)}, f32[2,4,96,768]{3...) custom-call(bf16[4,3,128,768]{3,2,1,0:T(8,128)(2,1)} %bitcast.70, ...), custom_call_target="tpu_custom_call" | custom-call | tf_op jit(solution)/shard_map/back/pallas_call | solution.py:1627
  371.4 0.9 slice_bitcast_fusion.1
  372.2 0.7 slice.69
  373.0 0.8 slice_reduce_fusion.2
  373.8 0.7 dynamic_slice.11
  374.5 0.6 fusion.17
  375.1 0.7 fusion.16
  375.8 3.4 copy.49
  379.2 1.4 copy.50
  380.6 1.2 copy.51
  381.8 0.8 copy.52
  382.6 1.4 copy.53
  384.0 1.4 copy.54
  (45 shorter events, 0.3 us)
Async XLA Ops:
  158.0 5.0 %copy-start.6 = (f32[4,384,128]{2,1,0:T(8,128)S(1)}, f32[4,384,128]{2,1,0:T(8,128)}, u32[]{:S(2)}) copy-start(f32[4,384,128]{2,1,0:T(8,128)} %get-tuple-element.46) | copy-start | bytes 2359300
  158.0 6.1 %copy-start.8 = (f32[4,16,256]{2,1,0:T(8,128)S(1)}, f32[4,16,256]{2,1,0:T(8,128)}, u32[]{:S(2)}) copy-start(f32[4,16,256]{2,1,0:T(8,128)} %get-tuple-element.52) | copy-start | bytes 196612
  158.0 70.9 %all-to-all-start = ((bf16[12,128,768]{2,1,0:T(8,128)(2,1)}), bf16[12,128,768]{2,1,0:T(8,128)(2,1)}, u32[]{:S(2)}, u32[]{:S(2)}) async-start(bf16[12,128,768]{2,1,0:T(8,128)(2,1)} %bitcast.71), calls=%async_computation | async-start | bytes 4718592 | tf_op jit(solution)/shard_map/all_to_all | solution.py:1739
  164.2 27.7 %slice-start = ((s8[4718592]{0:T(1024)(128)(4,1)}), s8[4194304]{0:T(1024)(128)(4,1)S(1)}, s32[]{:S(2)}) async-start(s8[4718592]{0:T(1024)(128)(4,1)} %bitcast.68), calls=%async_computation.1 | async-start | bytes 8388608
  176.7 15.3 %slice-start.1 = ((s8[4718592]{0:T(1024)(128)(4,1)}), s8[524288]{0:T(1024)(128)(4,1)S(1)}, s32[]{:S(2)}) async-start(s8[4718592]{0:T(1024)(128)(4,1)} %bitcast.68), calls=%async_computation.2 | async-start | bytes 1048576
  188.3 3.6 copy-start.1
  205.9 3.4 copy-start.9
  209.2 3.1 copy-start
  209.3 3.1 copy-start.10
  371.4 7.8 %copy-start.4 = (bf16[12,128,768]{2,1,0:T(8,128)(2,1)S(1)}, bf16[12,128,768]{2,1,0:T(8,128)(2,1)}, u32[]{:S(2)}) copy-start(bf16[12,128,768]{2,1,0:T(8,128)(2,1)} %get-tuple-element.113) | copy-start | bytes 7077892
  375.8 4.8 %copy-start.5 = (f32[192,2304]{1,0:T(8,128)S(1)}, f32[192,2304]{1,0:T(8,128)}, u32[]{:S(2)}) copy-start(f32[192,2304]{1,0:T(8,128)} %get-tuple-element.114) | copy-start | bytes 5308420
  379.2 2.6 copy-start.7
  379.2 3.4 copy-start.3
  380.6 3.4 copy-start.2
